TPU v7x, 32 devices: a whole 2x2x4 slice. The times are simulated.
32 devices in a mesh: ctx: 16 (over z, x, core), head: 2 (over y).
Axes of the slice: x: 2, y: 2, z: 4, core: 2. Of those that a mesh axis runs over, the one named last changes fastest.
Arguments:
- queries: bfloat16 [4096, 64, 128], P(('ctx', 'head')), may hold values from -112 to 112
- key_heads: bfloat16 [4096, 8, 128], P(('ctx', 'head')), may hold values from -5 to 5
- head_values: bfloat16 [4096, 8, 128], P(('ctx', 'head')), may hold values from -6 to 6
- output_gradient: bfloat16 [4096, 64, 128], P(('ctx', 'head')), may hold values from -6 to 6
- doc_lengths: int32 [8], replicated, may hold values from 1 to 1024, 4096 in all
Outputs:
- attended: bfloat16 [4096, 64, 128], P(('ctx', 'head'))
- grad_queries: bfloat16 [4096, 64, 128], P(('ctx', 'head'))
- grad_keys: bfloat16 [4096, 8, 128], P(('ctx', 'head'))
- grad_values: bfloat16 [4096, 8, 128], P(('ctx', 'head'))
Inputs may be any that keep to these rules, and one draw needn't show every extreme that they name: `doc_lengths`: the documents lie end to end and fill the sequence; the longest has exactly 1024 tokens.
All inputs are finite; a program needn't handle non-finite values.
Results may differ from a plain program's by a relative error of at most 0.0094.
Values may be sent and summed in bfloat16 or wider, within the bound.
A program may use at most 64 MiB of HBM per device.

v0:
```python
import jax
import jax.numpy as jnp
from jax import lax
from jax.sharding import PartitionSpec as P

MOST = 1024


def shifted(block, axis, distance):
    devices = range(lax.axis_size(axis))
    route = [(i - distance, i) for i in devices if i - distance in devices]
    return lax.ppermute(block, axis, route)


def document_starts(doc_lengths, positions):
    doc_ends = jnp.cumsum(doc_lengths)
    earlier = jnp.where(doc_ends[None, :] <= positions[:, None], doc_lengths[None, :], 0)
    return jnp.sum(earlier, axis=1)


def contract_last(left, right):
    return lax.dot_general(
        left, right, (((1,), (1,)), ((), ())), preferred_element_type=jnp.float32
    )


def contract_first(left, right):
    return lax.dot_general(
        left, right, (((0,), (0,)), ((), ())), preferred_element_type=jnp.float32
    )


def body(queries, key_heads, head_values, output_gradient, doc_lengths):
    queries, key_heads, head_values, output_gradient = (
        lax.all_to_all(queries, "head", split_axis=1, concat_axis=0, tiled=True),
        lax.all_to_all(key_heads, "head", split_axis=1, concat_axis=0, tiled=True),
        lax.all_to_all(head_values, "head", split_axis=1, concat_axis=0, tiled=True),
        lax.all_to_all(output_gradient, "head", split_axis=1, concat_axis=0, tiled=True),
    )
    row_count = queries.shape[0]
    head_count = queries.shape[1]
    kv_count = key_heads.shape[1]
    size_head = queries.shape[2]
    query_group_width = head_count // kv_count
    reach_steps = (MOST + row_count - 2) // row_count
    rows_in_window = reach_steps * row_count
    span_rows = rows_in_window + row_count
    score_scale = size_head ** (-0.5)
    leading_row = lax.axis_index("ctx") * row_count
    query_pos = leading_row + jnp.arange(row_count, dtype=jnp.int32)
    key_pos = leading_row - rows_in_window + jnp.arange(span_rows, dtype=jnp.int32)
    query_start = document_starts(doc_lengths, query_pos)
    allowed = (key_pos[None, :] >= query_start[:, None]) & (key_pos[None, :] <= query_pos[:, None])
    key_tiles = [key_heads]
    value_tiles = [head_values]
    current = (key_heads, head_values)
    for step_index in range(reach_steps):
        current = shifted((current[0], current[1]), "ctx", 1)
        key_tiles.insert(0, current[0])
        value_tiles.insert(0, current[1])
    key_window = jnp.concatenate(key_tiles, 0)
    value_window = jnp.concatenate(value_tiles, 0)
    head_ids = jnp.arange(head_count, dtype=jnp.int32)

    def scores_of(head_index):
        query_rows = lax.dynamic_index_in_dim(queries, head_index, 1, keepdims=False)
        key_rows = lax.dynamic_index_in_dim(
            key_window, head_index // query_group_width, 1, keepdims=False
        )
        value_rows = lax.dynamic_index_in_dim(
            value_window, head_index // query_group_width, 1, keepdims=False
        )
        scores = contract_last(query_rows, key_rows) * score_scale
        return (query_rows, key_rows, value_rows, scores)

    def forward_head(head_index):
        query_rows, key_rows, value_rows, scores = scores_of(head_index)
        masked = jnp.where(allowed, scores, -jnp.inf)
        row_max = jnp.max(masked, axis=-1, keepdims=True)
        row_total = jnp.sum(jnp.exp(masked - row_max), axis=-1, keepdims=True)
        log_total = row_max + jnp.log(row_total)
        probabilities = jnp.where(allowed, jnp.exp(scores - log_total), 0.0)
        attended_rows = jnp.dot(
            probabilities.astype(jnp.bfloat16), value_rows, preferred_element_type=jnp.float32
        ).astype(jnp.bfloat16)
        return (attended_rows, log_total)

    attended, log_totals = lax.map(forward_head, head_ids)
    attended_groups = attended.reshape(kv_count, query_group_width, row_count, size_head)
    log_groups = log_totals.reshape(kv_count, query_group_width, row_count, 1)

    def backward_group(inputs):
        kv_index, attended_set, log_set = inputs

        def one_head(sums, member):
            key_acc, value_acc = sums
            head_index = kv_index * query_group_width + member
            query_rows, key_rows, value_rows, scores = scores_of(head_index)
            attended_rows = lax.dynamic_index_in_dim(attended_set, member, 0, keepdims=False)
            log_total = lax.dynamic_index_in_dim(log_set, member, 0, keepdims=False)
            grad_rows = lax.dynamic_index_in_dim(output_gradient, head_index, 1, keepdims=False)
            probabilities = jnp.where(allowed, jnp.exp(scores - log_total), 0.0)
            rounded = probabilities.astype(jnp.bfloat16)
            row_delta = jnp.sum(
                grad_rows.astype(jnp.float32) * attended_rows.astype(jnp.float32),
                axis=1,
                keepdims=True,
            )
            grad_weights = contract_last(grad_rows, value_rows)
            grad_scores = (probabilities * (grad_weights - row_delta)).astype(jnp.bfloat16)
            grad_query = (
                score_scale * jnp.dot(grad_scores, key_rows, preferred_element_type=jnp.float32)
            ).astype(jnp.bfloat16)
            key_acc = key_acc + score_scale * contract_first(grad_scores, query_rows)
            value_acc = value_acc + contract_first(rounded, grad_rows)
            return ((key_acc, value_acc), grad_query)

        empty = jnp.zeros((span_rows, size_head), jnp.float32)
        members = jnp.arange(query_group_width, dtype=jnp.int32)
        (key_acc, value_acc), grad_set = lax.scan(one_head, (empty, empty), members)
        return (grad_set, key_acc, value_acc)

    kv_ids = jnp.arange(kv_count, dtype=jnp.int32)
    grad_sets, key_sum, value_sum = lax.map(backward_group, (kv_ids, attended_groups, log_groups))
    grad_query = grad_sets.reshape(head_count, row_count, size_head)
    partials = jnp.transpose(jnp.stack([key_sum, value_sum], 0), (2, 0, 1, 3))

    def tile_of(position):
        return partials[position * row_count : (position + 1) * row_count]

    gathered = tile_of(0)
    for step_index in range(reach_steps):
        gathered = shifted(gathered, "ctx", -1) + tile_of(step_index + 1)
    grad_keys = gathered[:, 0].astype(jnp.bfloat16)
    grad_values = gathered[:, 1].astype(jnp.bfloat16)
    attended_out = jnp.transpose(attended, (1, 0, 2))
    grad_query_out = jnp.transpose(grad_query, (1, 0, 2))
    return (
        lax.all_to_all(attended_out, "head", split_axis=0, concat_axis=1, tiled=True),
        lax.all_to_all(grad_query_out, "head", split_axis=0, concat_axis=1, tiled=True),
        lax.all_to_all(grad_keys, "head", split_axis=0, concat_axis=1, tiled=True),
        lax.all_to_all(grad_values, "head", split_axis=0, concat_axis=1, tiled=True),
    )


def solution(mesh):
    in_specs = (
        P(("ctx", "head"), None, None),
        P(("ctx", "head"), None, None),
        P(("ctx", "head"), None, None),
        P(("ctx", "head"), None, None),
        P(),
    )
    out_specs = (
        P(("ctx", "head"), None, None),
        P(("ctx", "head"), None, None),
        P(("ctx", "head"), None, None),
        P(("ctx", "head"), None, None),
    )
    return jax.shard_map(body, mesh=mesh, in_specs=in_specs, out_specs=out_specs, check_vma=False)
```

profile of v0, /device:TPU:23, one launch (start us, length us, event | category | flops | bytes accessed | tf_op | source)
XLA Modules:
  0.0 1028.8 jit_solution(17629481101210628741)
XLA Ops:
  2.3 3.7 all-to-all-start.1
  9.4 4.6 all-to-all-start.2
  14.0 4.3 copy.49
  18.3 3.8 all-to-all-start
  22.1 5.8 collective-permute-start
  27.8 4.3 copy.57
  32.1 11.2 %all-to-all-done = bf16[128,64,128]{2,0,1:T(8,128)(2,1)S(1)} async-done(((bf16[128,64,128]{2,0,1:T(8,128)(2,1)}), bf16[128,64,128]{2,0,1:T(8,128)(2,1)S(1)}, u32[]{:S(2)}, u32[]{:S(2)}) %all-to-all-start) | async-done | bytes 2097184 | tf_op jit(solution)/shard_map/all_to_all | solution.py:35
  43.3 6.0 all-to-all-start.4
  49.3 6.7 collective-permute-start.4
  59.3 5.3 collective-permute-start.5
  64.6 2.9 collective-permute-start.2
  67.9 5.3 collective-permute-start.6
  73.2 3.2 collective-permute-start.3
  76.7 5.1 collective-permute-start.7
  83.3 3.2 copy.58
  98.8 273.8 %while.63 = (s32[]{:T(128)}, bf16[32,256,128]{2,1,0:T(8,128)(2,1)}, f32[32,256,1]{1,2,0:T(1,128)}, s32[32]{0:T(128)S(1)}, bf16[256,32,128]{2,0,1:T(8,128)(2,1)},...) while((s32[]{:T(128)}, bf16[32,256,128]{2,1,0:T(8,128)(2,1)}, ...), condition=%wide.region_5.6_spmd.clone, body=%wide.region_2.5_spmd.clone.sunk | while | flops 173702944 | bytes 4750726 | solution.py:88
  104.7 2.1 fusion.75
  113.3 2.1 fusion.75
  121.8 2.1 fusion.75
  130.4 2.1 fusion.75
  138.9 2.1 fusion.75
  147.5 2.1 fusion.75
  156.0 2.1 fusion.75
  372.6 540.1 %while.65 = (s32[]{:T(128)}, bf16[4,8,256,128]{3,1,0,2:T(8,128)(2,1)}, f32[4,1280,128]{2,0,1:T(4,128)}, f32[4,1280,128]{2,0,1:T(4,128)}, bf16[4,8,256,128]{3,2,1...) while((s32[]{:T(128)}, ...), condition=%wide.region_10.11_spmd.clone, body=%wide.region_6.10_spmd.clone.sunk | while | flops 423722784 | bytes 20084772 | solution.py:124
  376.8 94.2 %while.66 = (s32[]{:T(128)}, f32[1280,128]{1,0:T(8,128)S(1)}, f32[1280,128]{1,0:T(8,128)S(1)}, bf16[8,256,128]{2,1,0:T(8,128)(2,1)}, s32[8]{0:T(128)S(1)}, /*ind...) while((s32[]{:T(128)}, f32[1280,128]{1,0:T(8,128)S(1)}, ...), condition=%wide.region_9.9_spmd.clone, body=%wide.region_7.8_spmd.clone.sunk | while | flops 422739744 | bytes 12916787 | solution.py:120
  471.0 17.8 %dynamic_update_slice.60 = f32[4,1280,128]{2,0,1:T(4,128)} dynamic-update-slice(f32[4,1280,128]{2,0,1:T(4,128)} %get-tuple-element.1054, f32[1,1280,128]{2,0,1:T(1,128)S(1)} %bitcast.163, s32[]{:T(128)} %get-tuple-element.1052, s32[]{:T(128)} %constant.215.clone.1..sunk.1, s32[]{:T(128)} %constant.215.clone.1..sunk.1) | dynamic-update-slice | bytes 1310724 | tf_op jit(solution)/shard_map/while/body/jit(dynamic_update_index_in_dim)/dynamic_update_slice | solution.py:124
  488.8 17.7 %dynamic_update_slice.61 = f32[4,1280,128]{2,0,1:T(4,128)} dynamic-update-slice(f32[4,1280,128]{2,0,1:T(4,128)} %get-tuple-element.1055, f32[1,1280,128]{2,0,1:T(1,128)S(1)} %bitcast.164, s32[]{:T(128)} %get-tuple-element.1052, s32[]{:T(128)} %constant.215.clone.1..sunk.1, s32[]{:T(128)} %constant.215.clone.1..sunk.1) | dynamic-update-slice | bytes 1310724 | tf_op jit(solution)/shard_map/while/body/jit(dynamic_update_index_in_dim)/dynamic_update_slice | solution.py:124
  511.9 94.2 %while.66 = (s32[]{:T(128)}, f32[1280,128]{1,0:T(8,128)S(1)}, f32[1280,128]{1,0:T(8,128)S(1)}, bf16[8,256,128]{2,1,0:T(8,128)(2,1)}, s32[8]{0:T(128)S(1)}, /*ind...) while((s32[]{:T(128)}, f32[1280,128]{1,0:T(8,128)S(1)}, ...), condition=%wide.region_9.9_spmd.clone, body=%wide.region_7.8_spmd.clone.sunk | while | flops 422739744 | bytes 12916787 | solution.py:120
  606.0 17.8 %dynamic_update_slice.60 = f32[4,1280,128]{2,0,1:T(4,128)} dynamic-update-slice(f32[4,1280,128]{2,0,1:T(4,128)} %get-tuple-element.1054, f32[1,1280,128]{2,0,1:T(1,128)S(1)} %bitcast.163, s32[]{:T(128)} %get-tuple-element.1052, s32[]{:T(128)} %constant.215.clone.1..sunk.1, s32[]{:T(128)} %constant.215.clone.1..sunk.1) | dynamic-update-slice | bytes 1310724 | tf_op jit(solution)/shard_map/while/body/jit(dynamic_update_index_in_dim)/dynamic_update_slice | solution.py:124
  623.8 17.7 %dynamic_update_slice.61 = f32[4,1280,128]{2,0,1:T(4,128)} dynamic-update-slice(f32[4,1280,128]{2,0,1:T(4,128)} %get-tuple-element.1055, f32[1,1280,128]{2,0,1:T(1,128)S(1)} %bitcast.164, s32[]{:T(128)} %get-tuple-element.1052, s32[]{:T(128)} %constant.215.clone.1..sunk.1, s32[]{:T(128)} %constant.215.clone.1..sunk.1) | dynamic-update-slice | bytes 1310724 | tf_op jit(solution)/shard_map/while/body/jit(dynamic_update_index_in_dim)/dynamic_update_slice | solution.py:124
  646.9 94.2 %while.66 = (s32[]{:T(128)}, f32[1280,128]{1,0:T(8,128)S(1)}, f32[1280,128]{1,0:T(8,128)S(1)}, bf16[8,256,128]{2,1,0:T(8,128)(2,1)}, s32[8]{0:T(128)S(1)}, /*ind...) while((s32[]{:T(128)}, f32[1280,128]{1,0:T(8,128)S(1)}, ...), condition=%wide.region_9.9_spmd.clone, body=%wide.region_7.8_spmd.clone.sunk | while | flops 422739744 | bytes 12916787 | solution.py:120
  741.1 17.8 %dynamic_update_slice.60 = f32[4,1280,128]{2,0,1:T(4,128)} dynamic-update-slice(f32[4,1280,128]{2,0,1:T(4,128)} %get-tuple-element.1054, f32[1,1280,128]{2,0,1:T(1,128)S(1)} %bitcast.163, s32[]{:T(128)} %get-tuple-element.1052, s32[]{:T(128)} %constant.215.clone.1..sunk.1, s32[]{:T(128)} %constant.215.clone.1..sunk.1) | dynamic-update-slice | bytes 1310724 | tf_op jit(solution)/shard_map/while/body/jit(dynamic_update_index_in_dim)/dynamic_update_slice | solution.py:124
  758.8 17.7 %dynamic_update_slice.61 = f32[4,1280,128]{2,0,1:T(4,128)} dynamic-update-slice(f32[4,1280,128]{2,0,1:T(4,128)} %get-tuple-element.1055, f32[1,1280,128]{2,0,1:T(1,128)S(1)} %bitcast.164, s32[]{:T(128)} %get-tuple-element.1052, s32[]{:T(128)} %constant.215.clone.1..sunk.1, s32[]{:T(128)} %constant.215.clone.1..sunk.1) | dynamic-update-slice | bytes 1310724 | tf_op jit(solution)/shard_map/while/body/jit(dynamic_update_index_in_dim)/dynamic_update_slice | solution.py:124
  781.9 94.2 %while.66 = (s32[]{:T(128)}, f32[1280,128]{1,0:T(8,128)S(1)}, f32[1280,128]{1,0:T(8,128)S(1)}, bf16[8,256,128]{2,1,0:T(8,128)(2,1)}, s32[8]{0:T(128)S(1)}, /*ind...) while((s32[]{:T(128)}, f32[1280,128]{1,0:T(8,128)S(1)}, ...), condition=%wide.region_9.9_spmd.clone, body=%wide.region_7.8_spmd.clone.sunk | while | flops 422739744 | bytes 12916787 | solution.py:120
  876.1 17.8 %dynamic_update_slice.60 = f32[4,1280,128]{2,0,1:T(4,128)} dynamic-update-slice(f32[4,1280,128]{2,0,1:T(4,128)} %get-tuple-element.1054, f32[1,1280,128]{2,0,1:T(1,128)S(1)} %bitcast.163, s32[]{:T(128)} %get-tuple-element.1052, s32[]{:T(128)} %constant.215.clone.1..sunk.1, s32[]{:T(128)} %constant.215.clone.1..sunk.1) | dynamic-update-slice | bytes 1310724 | tf_op jit(solution)/shard_map/while/body/jit(dynamic_update_index_in_dim)/dynamic_update_slice | solution.py:124
  893.9 17.7 %dynamic_update_slice.61 = f32[4,1280,128]{2,0,1:T(4,128)} dynamic-update-slice(f32[4,1280,128]{2,0,1:T(4,128)} %get-tuple-element.1055, f32[1,1280,128]{2,0,1:T(1,128)S(1)} %bitcast.164, s32[]{:T(128)} %get-tuple-element.1052, s32[]{:T(128)} %constant.215.clone.1..sunk.1, s32[]{:T(128)} %constant.215.clone.1..sunk.1) | dynamic-update-slice | bytes 1310724 | tf_op jit(solution)/shard_map/while/body/jit(dynamic_update_index_in_dim)/dynamic_update_slice | solution.py:124
  912.8 6.1 maximum_bitcast_fusion
  922.1 15.1 %collective-permute-done.8 = f32[256,2,4,128]{3,2,0,1:T(4,128)S(1)} collective-permute-done((f32[256,2,4,128]{3,2,0,1:T(4,128)S(1)}, f32[256,2,4,128]{3,2,0,1:T(4,128)S(1)}, u32[]{:S(2)}, u32[]{:S(2)}) %collective-permute-start.8) | collective-permute-done | bytes 1048608 | tf_op jit(solution)/shard_map/ppermute | solution.py:12
  940.8 14.9 %collective-permute-done.9 = f32[256,2,4,128]{3,2,0,1:T(4,128)S(1)} collective-permute-done((f32[256,2,4,128]{3,2,0,1:T(4,128)S(1)}, f32[256,2,4,128]{3,2,0,1:T(4,128)S(1)}, u32[]{:S(2)}, u32[]{:S(2)}) %collective-permute-start.9) | collective-permute-done | bytes 1048608 | tf_op jit(solution)/shard_map/ppermute | solution.py:12
  959.2 3.8 all-to-all-start.5
  962.9 11.4 %collective-permute-done.10 = f32[256,2,4,128]{3,2,0,1:T(4,128)} collective-permute-done((f32[256,2,4,128]{3,2,0,1:T(4,128)S(1)}, f32[256,2,4,128]{3,2,0,1:T(4,128)}, u32[]{:S(2)}, u32[]{:S(2)}) %collective-permute-start.10) | collective-permute-done | bytes 1048608 | tf_op jit(solution)/shard_map/ppermute | solution.py:12
  978.1 4.3 copy.73
  982.5 6.6 all-to-all-start.3
  989.1 4.2 collective-permute-done.11
  996.0 13.9 %all-to-all-done.3 = bf16[256,32,128]{2,1,0:T(8,128)(2,1)} async-done(((bf16[256,32,128]{2,1,0:T(8,128)(2,1)}), bf16[256,32,128]{2,1,0:T(8,128)(2,1)}, u32[]{:S(2)}, u32[]{:S(2)}) %all-to-all-start.3) | async-done | bytes 2097184 | tf_op jit(solution)/shard_map/all_to_all | solution.py:139
  1009.9 6.7 all_to_all.144
  1016.6 4.9 all-to-all-start.7
  1023.5 3.6 copy.56
  (668 shorter events, 510.4 us)
Async XLA Ops:
  2.3 7.1 all-to-all-start.1
  9.4 8.8 all-to-all-start.2
  18.3 25.0 %all-to-all-start = ((bf16[128,64,128]{2,0,1:T(8,128)(2,1)}), bf16[128,64,128]{2,0,1:T(8,128)(2,1)S(1)}, u32[]{:S(2)}, u32[]{:S(2)}) async-start(bf16[128,64,128]{2,0,1:T(8,128)(2,1)} %copy.49), calls=%async_computation | async-start | bytes 4194304 | tf_op jit(solution)/shard_map/all_to_all | solution.py:35
  22.1 33.9 %collective-permute-start = (bf16[256,4,128]{2,0,1:T(8,128)(2,1)S(1)}, bf16[256,4,128]{2,0,1:T(8,128)(2,1)S(1)}, u32[]{:S(2)}, u32[]{:S(2)}) collective-permute-start(bf16[256,4,128]{2,0,1:T(8,128)(2,1)S(1)} %bitcast.176), channel_id=1, source_target_pairs={{0,2},{2,4},{4,6},{6,8},{8,10},{10,12},{12,14},{14,16},{16,18},{18... | collective-permute-start | bytes 786440 | tf_op jit(solution)/shard_map/ppermute | solution.py:12
  32.1 44.3 %copy-start.3 = (s32[8]{0:T(128)S(1)}, s32[8]{0:T(128)}, u32[]{:S(2)}) copy-start(s32[8]{0:T(128)} %param.15) | copy-start | bytes 100
  43.3 40.0 %all-to-all-start.4 = ((bf16[128,64,128]{2,0,1:T(8,128)(2,1)}), bf16[128,64,128]{2,0,1:T(8,128)(2,1)}, u32[]{:S(2)}, u32[]{:S(2)}) async-start(bf16[128,64,128]{2,0,1:T(8,128)(2,1)} %copy.57), calls=%async_computation.4 | async-start | bytes 4194304 | tf_op jit(solution)/shard_map/all_to_all | solution.py:38
  49.3 10.0 collective-permute-start.4
  56.0 8.6 collective-permute-start.1
  59.3 8.6 collective-permute-start.5
  64.6 8.6 collective-permute-start.2
  67.9 8.9 collective-permute-start.6
  73.2 13.3 %collective-permute-start.3 = (bf16[256,4,128]{2,0,1:T(8,128)(2,1)}, bf16[256,4,128]{2,0,1:T(8,128)(2,1)}, u32[]{:S(2)}, u32[]{:S(2)}) collective-permute-start(bf16[256,4,128]{2,0,1:T(8,128)(2,1)} %collective-permute-done.2), channel_id=1, source_target_pairs={{0,2},{2,4},{4,6},{6,8},{8,10},{10,12},{12,14},{14,16},{16,18},{18... | collective-permute-start | bytes 786440 | tf_op jit(solution)/shard_map/ppermute | solution.py:12
  76.7 16.4 %collective-permute-start.7 = (bf16[256,4,128]{2,0,1:T(8,128)(2,1)}, bf16[256,4,128]{2,0,1:T(8,128)(2,1)}, u32[]{:S(2)}, u32[]{:S(2)}) collective-permute-start(bf16[256,4,128]{2,0,1:T(8,128)(2,1)} %collective-permute-done.6), channel_id=1, source_target_pairs={{0,2},{2,4},{4,6},{6,8},{8,10},{10,12},{12,14},{14,16},{16,18},{18... | collective-permute-start | bytes 786440 | tf_op jit(solution)/shard_map/ppermute | solution.py:12
  376.8 5.6 copy-start
  388.6 5.6 copy-start
  400.4 5.6 copy-start
  412.2 5.6 copy-start
  423.9 5.6 copy-start
  435.7 5.6 copy-start
  447.5 5.6 copy-start
  471.0 35.5 %copy-start.2 = (bf16[8,256,128]{2,1,0:T(8,128)(2,1)S(1)}, bf16[8,256,128]{2,1,0:T(8,128)(2,1)}, u32[]{:S(2)}) copy-start(bf16[8,256,128]{2,1,0:T(8,128)(2,1)} %get-tuple-element.898) | copy-start | bytes 1572868 | tf_op jit(solution)/shard_map/while
  511.9 5.6 copy-start
  523.6 5.6 copy-start
  547.2 5.6 copy-start
  559.0 5.6 copy-start
  570.7 5.6 copy-start
  582.5 5.6 copy-start
  606.0 35.5 %copy-start.2 = (bf16[8,256,128]{2,1,0:T(8,128)(2,1)S(1)}, bf16[8,256,128]{2,1,0:T(8,128)(2,1)}, u32[]{:S(2)}) copy-start(bf16[8,256,128]{2,1,0:T(8,128)(2,1)} %get-tuple-element.898) | copy-start | bytes 1572868 | tf_op jit(solution)/shard_map/while
  646.9 5.6 copy-start
  658.7 5.6 copy-start
  670.4 5.6 copy-start
  682.2 5.6 copy-start
  705.8 5.6 copy-start
  717.5 5.6 copy-start
  741.1 35.5 %copy-start.2 = (bf16[8,256,128]{2,1,0:T(8,128)(2,1)S(1)}, bf16[8,256,128]{2,1,0:T(8,128)(2,1)}, u32[]{:S(2)}) copy-start(bf16[8,256,128]{2,1,0:T(8,128)(2,1)} %get-tuple-element.898) | copy-start | bytes 1572868 | tf_op jit(solution)/shard_map/while
  793.7 5.6 copy-start
  805.5 5.6 copy-start
  817.2 5.6 copy-start
  840.8 5.6 copy-start
  852.6 5.6 copy-start
  876.1 35.5 %copy-start.2 = (bf16[8,256,128]{2,1,0:T(8,128)(2,1)S(1)}, bf16[8,256,128]{2,1,0:T(8,128)(2,1)}, u32[]{:S(2)}) copy-start(bf16[8,256,128]{2,1,0:T(8,128)(2,1)} %get-tuple-element.898) | copy-start | bytes 1572868 | tf_op jit(solution)/shard_map/while
  920.2 17.0 %collective-permute-start.8 = (f32[256,2,4,128]{3,2,0,1:T(4,128)S(1)}, f32[256,2,4,128]{3,2,0,1:T(4,128)S(1)}, u32[]{:S(2)}, u32[]{:S(2)}) collective-permute-start(f32[256,2,4,128]{3,2,0,1:T(4,128)S(1)} %slice.30), channel_id=1, source_target_pairs={{2,0},{4,2},{6,4},{8,6},{10,8},{12,10},{14,12},{16,14},{18,16},{20... | collective-permute-start | bytes 3145736 | tf_op jit(solution)/shard_map/ppermute | solution.py:12
  938.7 17.0 %collective-permute-start.9 = (f32[256,2,4,128]{3,2,0,1:T(4,128)S(1)}, f32[256,2,4,128]{3,2,0,1:T(4,128)S(1)}, u32[]{:S(2)}, u32[]{:S(2)}) collective-permute-start(f32[256,2,4,128]{3,2,0,1:T(4,128)S(1)} %slice_add_fusion.3), channel_id=1, source_target_pairs={{2,0},{4,2},{6,4},{8,6},{10,8},{12,10},{14,12},{16,14},{18,16},{20... | collective-permute-start | bytes 3145736 | tf_op jit(solution)/shard_map/ppermute | solution.py:12
  957.2 17.1 %collective-permute-start.10 = (f32[256,2,4,128]{3,2,0,1:T(4,128)S(1)}, f32[256,2,4,128]{3,2,0,1:T(4,128)}, u32[]{:S(2)}, u32[]{:S(2)}) collective-permute-start(f32[256,2,4,128]{3,2,0,1:T(4,128)S(1)} %slice_add_fusion.2), channel_id=1, source_target_pairs={{2,0},{4,2},{6,4},{8,6},{10,8},{12,10},{14,12},{16,14},{18,16},{20... | collective-permute-start | bytes 3145736 | tf_op jit(solution)/shard_map/ppermute | solution.py:12
  959.2 23.4 %all-to-all-start.5 = ((bf16[256,32,128]{2,1,0:T(8,128)(2,1)}), bf16[256,32,128]{2,1,0:T(8,128)(2,1)S(1)}, u32[]{:S(2)}, u32[]{:S(2)}) async-start(bf16[256,32,128]{2,1,0:T(8,128)(2,1)} %bitcast.173), calls=%async_computation.5 | async-start | bytes 4194304 | tf_op jit(solution)/shard_map/all_to_all | solution.py:140
  976.2 17.1 %collective-permute-start.11 = (f32[256,2,4,128]{3,2,0,1:T(4,128)S(1)}, f32[256,2,4,128]{3,2,0,1:T(4,128)}, u32[]{:S(2)}, u32[]{:S(2)}) collective-permute-start(f32[256,2,4,128]{3,2,0,1:T(4,128)S(1)} %slice_add_fusion.1), channel_id=1, source_target_pairs={{2,0},{4,2},{6,4},{8,6},{10,8},{12,10},{14,12},{16,14},{18,16},{20... | collective-permute-start | bytes 3145736 | tf_op jit(solution)/shard_map/ppermute | solution.py:12
  982.5 27.4 %all-to-all-start.3 = ((bf16[256,32,128]{2,1,0:T(8,128)(2,1)}), bf16[256,32,128]{2,1,0:T(8,128)(2,1)}, u32[]{:S(2)}, u32[]{:S(2)}) async-start(bf16[256,32,128]{2,1,0:T(8,128)(2,1)} %bitcast.169), calls=%async_computation.3 | async-start | bytes 4194304 | tf_op jit(solution)/shard_map/all_to_all | solution.py:139
  1016.6 11.4 %all-to-all-start.7 = ((bf16[256,4,128]{2,1,0:T(4,128)(2,1)}), bf16[256,4,128]{2,1,0:T(4,128)(2,1)S(1)}, u32[]{:S(2)}, u32[]{:S(2)}) async-start(bf16[256,4,128]{2,1,0:T(4,128)(2,1)} %get-tuple-element.649), calls=%async_computation.7 | async-start | bytes 524288 | tf_op jit(solution)/shard_map/all_to_all | solution.py:142
  (40 other events, 90.8 us)
where the time goes:
time: 1050 us; the launch traced here: 1030 us
  matrix products  358 us (34%)
  local copies, waits for them, and re-layouts  259 us (25%)
  loops' own time  190 us (18%)
  starting transfers between devices  77.2 us (7%)
  waiting for transfers between devices  74.4 us (7%)
  other arithmetic  62.5 us (6%)
    dynamic_update_slice x12, local copies, waits for them, and re-layouts, body(): lax.map(backward_group, (kv_ids, attended_groups, log_groups))  147 us
    dot_general x96, matrix products, contract_last(): lax.dot_general(left, right, (((1,), (1,)), ((), ())), preferred_element_...  139 us
    another operation x1, loops' own time, body(): attended, log_totals = lax.map(forward_head, head_ids)  106 us
    dot_general x64, matrix products, contract_first(): lax.dot_general(left, right, (((0,), (0,)), ((), ())), preferred_element_...  89.6 us
    another operation x4, loops' own time, backward_group(): (key_acc, value_acc), grad_set = lax.scan(one_head, (empty, empty), members)  81.8 us
    dot_general x32, matrix products, forward_head(): jnp.dot(probabilities.astype(jnp.bfloat16), value_rows, preferred_element...  67.5 us
    dot_general x32, matrix products, one_head(): jnp.dot(grad_scores, key_rows, preferred_element_type=jnp.float32)  61.8 us
    ppermute x12, waiting for transfers between devices, shifted(): return lax.ppermute(block, axis, route)  47.3 us
  transfers between devices with their start and end apart: 19, of which 10 were waited for; matrix products, arithmetic and copies ran while one was open for 4% of the time, Pallas kernels for 0%

commit v1 on v0

v1 whole, which is shorter than its diff:
```python
import functools

import jax
import jax.numpy as jnp
from jax import lax
from jax.experimental import pallas as pl
from jax.experimental.pallas import tpu as pltpu
from jax.sharding import PartitionSpec as P

MOST = 1024
AXES = ("ctx", "head")
MASKED = -1e30


def document_starts(doc_lengths, positions):
    doc_ends = jnp.cumsum(doc_lengths)
    earlier = jnp.where(doc_ends[None, :] <= positions[:, None], doc_lengths[None, :], 0)
    return jnp.sum(earlier, axis=1)


def nt(left, right):
    return lax.dot_general(
        left, right, (((1,), (1,)), ((), ())), preferred_element_type=jnp.float32
    )


def nn(left, right):
    return jnp.dot(left, right, preferred_element_type=jnp.float32)


def attention_kernel(steps, rows, score_scale, *refs):
    bounds_ref, q_ref, do_ref = refs[:3]
    kv_refs = refs[3 : 4 + steps]
    o_ref, dq_ref = refs[4 + steps : 6 + steps]
    dkv_refs = refs[6 + steps : 7 + 2 * steps]
    bias, k_s, v_s, kt_s, vt_s, dk_s, dv_s = refs[7 + 2 * steps :]
    tokens, width, size_head = q_ref.shape
    span = (steps + 1) * tokens
    total_rows = tokens * width

    @pl.when(pl.program_id(0) == 0)
    def _():
        key_at = lax.broadcasted_iota(jnp.int32, (span, total_rows), 0)
        allowed = (key_at >= bounds_ref[0:1, :]) & (key_at <= bounds_ref[1:2, :])
        bias[...] = jnp.where(allowed, 0.0, MASKED)

    for i in range(steps + 1):
        at = pl.ds(i * tokens, tokens)
        k_s[at, :] = kv_refs[i][0]
        v_s[at, :] = kv_refs[i][1]
    kt_s[...] = k_s[...].T
    vt_s[...] = v_s[...].T
    dk_s[...] = jnp.zeros_like(dk_s)
    dv_s[...] = jnp.zeros_like(dv_s)
    part = rows // width

    @pl.loop(0, total_rows // rows)
    def _(c):
        toks = pl.ds(pl.multiple_of(c * part, part), part)
        lanes = pl.ds(pl.multiple_of(c * rows, rows), rows)
        q = q_ref[toks].reshape(rows, size_head)
        do = do_ref[toks].reshape(rows, size_head)
        x = nt(k_s[...], q) + bias[:, lanes]
        top = jnp.max(x, axis=0, keepdims=True)
        e = jnp.exp((x - top) * score_scale)
        inv = 1.0 / jnp.sum(e, axis=0, keepdims=True)
        p = e * inv
        w = p.astype(jnp.bfloat16)
        ot = nn(vt_s[...], w).astype(jnp.bfloat16)
        dot_f = do.T.astype(jnp.float32)
        delta = jnp.sum(dot_f * ot.astype(jnp.float32), axis=0, keepdims=True)
        o_ref[toks] = ot.T.reshape(part, width, size_head)
        dp = nt(v_s[...], do)
        ds = (p * (dp - delta)).astype(jnp.bfloat16)
        dv_s[...] += nn(w, do)
        dk_s[...] += nn(ds, q)
        dqt = (nn(kt_s[...], ds) * score_scale).astype(jnp.bfloat16)
        dq_ref[toks] = dqt.T.reshape(part, width, size_head)

    for i in range(steps + 1):
        at = pl.ds(i * tokens, tokens)
        dkv_refs[i][0] = (dk_s[at, :] * score_scale).astype(dkv_refs[i].dtype)
        dkv_refs[i][1] = dv_s[at, :].astype(dkv_refs[i].dtype)


def attention(queries, output_gradient, kv_blocks, bounds, score_scale):
    tokens, heads, size_head = queries.shape
    kv_count = kv_blocks[0].shape[1]
    width = heads // kv_count
    steps = len(kv_blocks) - 1
    span = (steps + 1) * tokens
    total_rows = tokens * width
    rows = min(256, total_rows)
    q4 = queries.reshape(tokens, kv_count, width, size_head)
    do4 = output_gradient.reshape(tokens, kv_count, width, size_head)
    row_spec = pl.BlockSpec((tokens, None, width, size_head), lambda g: (0, g, 0, 0))
    kv_spec = pl.BlockSpec((2, None, tokens, size_head), lambda g: (0, g, 0, 0))
    row_shape = jax.ShapeDtypeStruct(q4.shape, jnp.bfloat16)
    sent = jax.ShapeDtypeStruct(kv_blocks[0].shape, jnp.bfloat16)
    kept = jax.ShapeDtypeStruct(kv_blocks[0].shape, jnp.float32)
    outs = pl.pallas_call(
        functools.partial(attention_kernel, steps, rows, score_scale),
        grid=(kv_count,),
        in_specs=[pl.BlockSpec((2, total_rows), lambda g: (0, 0)), row_spec, row_spec]
        + [kv_spec] * (steps + 1),
        out_specs=[row_spec, row_spec] + [kv_spec] * (steps + 1),
        out_shape=[row_shape, row_shape] + [sent] * steps + [kept],
        scratch_shapes=[
            pltpu.VMEM((span, total_rows), jnp.float32),
            pltpu.VMEM((span, size_head), jnp.bfloat16),
            pltpu.VMEM((span, size_head), jnp.bfloat16),
            pltpu.VMEM((size_head, span), jnp.bfloat16),
            pltpu.VMEM((size_head, span), jnp.bfloat16),
            pltpu.VMEM((span, size_head), jnp.float32),
            pltpu.VMEM((span, size_head), jnp.float32),
        ],
        compiler_params=pltpu.CompilerParams(
            dimension_semantics=("arbitrary",), vmem_limit_bytes=56 << 20
        ),
        name="attention",
    )(bounds, q4, do4, *kv_blocks)
    return outs[0].reshape(queries.shape), outs[1].reshape(queries.shape), outs[2:]


def body(queries, key_heads, head_values, output_gradient, doc_lengths):
    tokens, heads, size_head = queries.shape
    width = heads // key_heads.shape[1]
    devices = lax.axis_size("ctx") * lax.axis_size("head")
    steps = (MOST + tokens - 2) // tokens
    base = (lax.axis_index("ctx") * lax.axis_size("head") + lax.axis_index("head")) * tokens
    query_pos = base + jnp.arange(tokens, dtype=jnp.int32)
    query_start = document_starts(doc_lengths, query_pos)
    window_base = base - steps * tokens
    bounds = jnp.stack([query_start, query_pos], 0) - window_base
    bounds = jnp.repeat(bounds, width, axis=1)

    own = jnp.transpose(jnp.stack([key_heads, head_values], 0), (0, 2, 1, 3))

    def moved(block, distance):
        route = [(i, (i + distance) % devices) for i in range(devices)]
        return lax.ppermute(block, AXES, route)

    blocks = [moved(own, s) for s in range(steps, 0, -1)] + [own]
    attended, grad_query, parts = attention(
        queries, output_gradient, blocks, bounds, size_head ** (-0.5)
    )
    total = parts[steps]
    for i in range(steps):
        total = total + moved(parts[i], i - steps).astype(jnp.float32)
    total = jnp.transpose(total.astype(jnp.bfloat16), (0, 2, 1, 3))
    return attended, grad_query, total[0], total[1]


def solution(mesh):
    whole = P(AXES, None, None)
    return jax.shard_map(
        body,
        mesh=mesh,
        in_specs=(whole, whole, whole, whole, P()),
        out_specs=(whole, whole, whole, whole),
        check_vma=False,
    )
```

time: 1050 us -> 210 us (0.20); the launches traced: 1030 us -> 207 us
  matrix products: 358 us -> 0 us
  local copies, waits for them, and re-layouts: 259 us -> 3.75 us
  loops' own time: 190 us -> 0 us
  Pallas kernels: 0 us -> 61.8 us
  starting transfers between devices: 77.2 us -> 16 us
  other arithmetic: 62.5 us -> 2.34 us
  waiting for transfers between devices: 74.4 us -> 123 us
    dot_general x224 -> x0, matrix products: 358 us -> none  [the longest x96 139 us: contract_last(): lax.dot_general(left, right, (((1,), (1,)), ((), ())), preferred_element_...]
    another operation x6 -> x0, loops' own time: 190 us -> none  [the longest x1 106 us: body(): attended, log_totals = lax.map(forward_head, head_ids)]
    dynamic_update_slice x44 -> x0, local copies, waits for them, and re-layouts: 165 us -> none  [the longest x12 147 us: body(): lax.map(backward_group, (kv_ids, attended_groups, log_groups))]
    ppermute x12 -> x16, waiting for transfers between devices: 47.3 us -> 123 us  [moved(): return lax.ppermute(block, AXES, route)]
    pallas_call x0 -> x1, Pallas kernels: none -> 61.8 us  [attention(): pl.pallas_call(functools.partial(attention_kernel, steps, rows, score_sca...]
    reduce_sum x64 -> x0, other arithmetic: 47.8 us -> none  [the longest x32 31.7 us: one_head(): jnp.sum(grad_rows.astype(jnp.float32) * attended_rows.astype(jnp.float32)...]
    dynamic_slice x100 -> x0, local copies, waits for them, and re-layouts: 40.8 us -> none  [the longest x32 20.5 us: backward_group(): (key_acc, value_acc), grad_set = lax.scan(one_head, (empty, empty), members)]
    all_to_all x7 -> x0, starting transfers between devices: 33.2 us -> none  [the longest x1 6.56 us: body(): lax.all_to_all(attended_out, 'head', split_axis=0, concat_axis=1, tiled=T...]
  transfers between devices with their start and end apart: 19 -> 16, of which waited for: 10 -> 14; matrix products, arithmetic and copies ran while one was open for 4% -> 1% of each run, Pallas kernels for 0% -> 0%
where the time goes in v1:
time: 210 us; the launch traced here: 207 us
  waiting for transfers between devices  123 us (59%)
  Pallas kernels  61.8 us (29%)
  starting transfers between devices  16 us (8%)
  local copies, waits for them, and re-layouts  3.75 us (2%)
  other arithmetic  2.34 us (1%)
    ppermute x16, waiting for transfers between devices, moved(): return lax.ppermute(block, AXES, route)  123 us
    pallas_call x1, Pallas kernels, attention(): pl.pallas_call(functools.partial(attention_kernel, steps, rows, score_sca...  61.8 us
    ppermute x16, starting transfers between devices, moved(): return lax.ppermute(block, AXES, route)  16 us
  transfers between devices with their start and end apart: 16, of which 14 were waited for; matrix products, arithmetic and copies ran while one was open for 1% of the time, Pallas kernels for 0%

profile of v1, /device:TPU:23, one launch (start us, length us, event | category | flops | bytes accessed | tf_op | source)
XLA Modules:
  0.0 207.4 jit_solution(13940499906085742958)
XLA Ops:
  0.6 0.0 copy-start.6
  0.6 1.1 copy_bitcast_fusion
  1.8 0.1 maximum_bitcast_fusion.refs_11_
  1.8 0.0 copy-start
  1.8 1.8 collective-permute-start.7
  3.7 0.1 collective-permute-start.6
  3.8 2.6 %collective-permute-start.5 = (bf16[2,8,128,128]{3,2,1,0:T(8,128)(2,1)S(1)}, bf16[2,8,128,128]{3,2,1,0:T(8,128)(2,1)S(1)}, u32[]{:S(2)}, u32[]{:S(2)}) collective-permute-start(bf16[2,8,128,128]{3,2,1,0:T(8,128)(2,1)S(1)} %maximum_bitcast_fusion.refs_11_), channel_id=1, source_target_pairs={{0,3},{1,4},{2,5},{3,6},{4,7},{5,8},{6,9},{7,10},{8,11},{9,12},{10... | collective-permute-start | bytes 1572872 | tf_op jit(solution)/shard_map/ppermute | solution.py:141
  6.4 0.0 collective-permute-start.4
  6.4 0.3 collective-permute-start.3
  6.7 10.0 %collective-permute-done.7.refs_10_ = bf16[2,8,128,128]{3,2,1,0:T(8,128)(2,1)S(1)} collective-permute-done((bf16[2,8,128,128]{3,2,1,0:T(8,128)(2,1)S(1)}, bf16[2,8,128,128]{3,2,1,0:T(8,128)(2,1)S(1)}, u32[]{:S(2)}, u32[]{:S(2)}) %collective-permute-start.7) | collective-permute-done | bytes 524320 | tf_op jit(solution)/shard_map/ppermute | solution.py:141
  16.7 5.0 %collective-permute-start.2 = (bf16[2,8,128,128]{3,2,1,0:T(8,128)(2,1)S(1)}, bf16[2,8,128,128]{3,2,1,0:T(8,128)(2,1)}, u32[]{:S(2)}, u32[]{:S(2)}) collective-permute-start(bf16[2,8,128,128]{3,2,1,0:T(8,128)(2,1)S(1)} %maximum_bitcast_fusion.refs_11_), channel_id=1, source_target_pairs={{0,6},{1,7},{2,8},{3,9},{4,10},{5,11},{6,12},{7,13},{8,14},{9,15},... | collective-permute-start | bytes 1572872 | tf_op jit(solution)/shard_map/ppermute | solution.py:141
  21.7 7.0 %collective-permute-done.6.refs_9_ = bf16[2,8,128,128]{3,2,1,0:T(8,128)(2,1)S(1)} collective-permute-done((bf16[2,8,128,128]{3,2,1,0:T(8,128)(2,1)S(1)}, bf16[2,8,128,128]{3,2,1,0:T(8,128)(2,1)S(1)}, u32[]{:S(2)}, u32[]{:S(2)}) %collective-permute-start.6) | collective-permute-done | bytes 524320 | tf_op jit(solution)/shard_map/ppermute | solution.py:141
  28.7 0.0 collective-permute-start.1
  28.7 14.9 %collective-permute-done.5.refs_8_ = bf16[2,8,128,128]{3,2,1,0:T(8,128)(2,1)S(1)} collective-permute-done((bf16[2,8,128,128]{3,2,1,0:T(8,128)(2,1)S(1)}, bf16[2,8,128,128]{3,2,1,0:T(8,128)(2,1)S(1)}, u32[]{:S(2)}, u32[]{:S(2)}) %collective-permute-start.5) | collective-permute-done | bytes 524320 | tf_op jit(solution)/shard_map/ppermute | solution.py:141
  43.7 0.0 collective-permute-start
  43.7 0.2 reduce-window.8
  43.9 0.1 select_reduce_fusion
  44.0 0.1 broadcast_in_dim.20
  44.1 0.7 reshape.61.refs_0_
  44.8 10.9 %collective-permute-done.4.refs_7_ = bf16[2,8,128,128]{3,2,1,0:T(8,128)(2,1)S(1)} collective-permute-done((bf16[2,8,128,128]{3,2,1,0:T(8,128)(2,1)S(1)}, bf16[2,8,128,128]{3,2,1,0:T(8,128)(2,1)S(1)}, u32[]{:S(2)}, u32[]{:S(2)}) %collective-permute-start.4) | collective-permute-done | bytes 524320 | tf_op jit(solution)/shard_map/ppermute | solution.py:141
  55.7 11.2 %collective-permute-done.3.refs_6_ = bf16[2,8,128,128]{3,2,1,0:T(8,128)(2,1)S(1)} collective-permute-done((bf16[2,8,128,128]{3,2,1,0:T(8,128)(2,1)S(1)}, bf16[2,8,128,128]{3,2,1,0:T(8,128)(2,1)S(1)}, u32[]{:S(2)}, u32[]{:S(2)}) %collective-permute-start.3) | collective-permute-done | bytes 524320 | tf_op jit(solution)/shard_map/ppermute | solution.py:141
  66.9 11.2 %collective-permute-done.2.refs_5_ = bf16[2,8,128,128]{3,2,1,0:T(8,128)(2,1)} collective-permute-done((bf16[2,8,128,128]{3,2,1,0:T(8,128)(2,1)S(1)}, bf16[2,8,128,128]{3,2,1,0:T(8,128)(2,1)}, u32[]{:S(2)}, u32[]{:S(2)}) %collective-permute-start.2) | collective-permute-done | bytes 524320 | tf_op jit(solution)/shard_map/ppermute | solution.py:141
  78.2 7.8 %collective-permute-done.1.refs_4_ = bf16[2,8,128,128]{3,2,1,0:T(8,128)(2,1)} collective-permute-done((bf16[2,8,128,128]{3,2,1,0:T(8,128)(2,1)S(1)}, bf16[2,8,128,128]{3,2,1,0:T(8,128)(2,1)}, u32[]{:S(2)}, u32[]{:S(2)}) %collective-permute-start.1) | collective-permute-done | bytes 524320 | tf_op jit(solution)/shard_map/ppermute | solution.py:141
  85.9 5.9 %collective-permute-done.refs_3_ = bf16[2,8,128,128]{3,2,1,0:T(8,128)(2,1)} collective-permute-done((bf16[2,8,128,128]{3,2,1,0:T(8,128)(2,1)S(1)}, bf16[2,8,128,128]{3,2,1,0:T(8,128)(2,1)}, u32[]{:S(2)}, u32[]{:S(2)}) %collective-permute-start) | collective-permute-done | bytes 524320 | tf_op jit(solution)/shard_map/ppermute | solution.py:141
  91.9 0.0 copy-done.2
  91.9 0.0 copy-done.3
  91.9 0.0 copy-done.4
  91.9 0.0 copy-done.5
  91.9 61.8 %attention.1 = (bf16[128,8,8,128]{3,2,1,0:T(8,128)(2,1)}, bf16[128,8,8,128]{3,2,1,0:T(8,128)(2,1)}, bf16[2,8,128,128]{3,2,1,0:T(8,128)(2,1)}, bf16[2,8,128,128]{...) custom-call(s32[2,1024]{1,0:T(2,128)} %reshape.61.refs_0_, ...), custom_call_target="tpu_custom_call" | custom-call | tf_op jit(solution)/shard_map/attention/pallas_call | solution.py:101
  153.7 0.4 collective-permute-start.8
  154.1 0.0 collective-permute-start.9
  154.1 0.0 collective-permute-start.10
  154.1 0.0 collective-permute-start.11
  154.1 5.8 %collective-permute-start.12 = (bf16[2,8,128,128]{3,2,1,0:T(8,128)(2,1)}, bf16[2,8,128,128]{3,2,1,0:T(8,128)(2,1)S(1)}, u32[]{:S(2)}, u32[]{:S(2)}) collective-permute-start(bf16[2,8,128,128]{3,2,1,0:T(8,128)(2,1)} %get-tuple-element.22), channel_id=1, source_target_pairs={{0,28},{1,29},{2,30},{3,31},{4,0},{5,1},{6,2},{7,3},{8,4},{9,5},{1... | collective-permute-start | bytes 1572872 | tf_op jit(solution)/shard_map/ppermute | solution.py:141
  159.9 8.3 %collective-permute-done.8 = bf16[2,8,128,128]{3,2,1,0:T(8,128)(2,1)S(1)} collective-permute-done((bf16[2,8,128,128]{3,2,1,0:T(8,128)(2,1)}, bf16[2,8,128,128]{3,2,1,0:T(8,128)(2,1)S(1)}, u32[]{:S(2)}, u32[]{:S(2)}) %collective-permute-start.8) | collective-permute-done | bytes 524320 | tf_op jit(solution)/shard_map/ppermute | solution.py:141
  168.2 0.0 collective-permute-start.13
  168.2 5.5 %collective-permute-done.9 = bf16[2,8,128,128]{3,2,1,0:T(8,128)(2,1)S(1)} collective-permute-done((bf16[2,8,128,128]{3,2,1,0:T(8,128)(2,1)}, bf16[2,8,128,128]{3,2,1,0:T(8,128)(2,1)S(1)}, u32[]{:S(2)}, u32[]{:S(2)}) %collective-permute-start.9) | collective-permute-done | bytes 524320 | tf_op jit(solution)/shard_map/ppermute | solution.py:141
  173.7 0.0 collective-permute-start.14
  173.7 1.1 collective-permute-done.10
  174.8 0.0 collective-permute-start.15
  174.8 11.3 %collective-permute-done.11 = bf16[2,8,128,128]{3,2,1,0:T(8,128)(2,1)S(1)} collective-permute-done((bf16[2,8,128,128]{3,2,1,0:T(8,128)(2,1)}, bf16[2,8,128,128]{3,2,1,0:T(8,128)(2,1)S(1)}, u32[]{:S(2)}, u32[]{:S(2)}) %collective-permute-start.11) | collective-permute-done | bytes 524320 | tf_op jit(solution)/shard_map/ppermute | solution.py:141
  186.1 11.2 %collective-permute-done.12 = bf16[2,8,128,128]{3,2,1,0:T(8,128)(2,1)S(1)} collective-permute-done((bf16[2,8,128,128]{3,2,1,0:T(8,128)(2,1)}, bf16[2,8,128,128]{3,2,1,0:T(8,128)(2,1)S(1)}, u32[]{:S(2)}, u32[]{:S(2)}) %collective-permute-start.12) | collective-permute-done | bytes 524320 | tf_op jit(solution)/shard_map/ppermute | solution.py:141
  197.3 0.0 collective-permute-done.13
  197.3 0.0 collective-permute-done.14
  197.3 6.2 %collective-permute-done.15 = bf16[2,8,128,128]{3,2,1,0:T(8,128)(2,1)S(1)} collective-permute-done((bf16[2,8,128,128]{3,2,1,0:T(8,128)(2,1)}, bf16[2,8,128,128]{3,2,1,0:T(8,128)(2,1)S(1)}, u32[]{:S(2)}, u32[]{:S(2)}) %collective-permute-start.15) | collective-permute-done | bytes 524320 | tf_op jit(solution)/shard_map/ppermute | solution.py:141
  203.6 2.0 fusion
  205.6 0.9 copy.20
  206.5 0.9 copy.19
  (12 shorter events, 0.1 us)
Async XLA Ops:
  0.6 43.1 %copy-start.6 = (s32[8]{0:T(128)S(1)}, s32[8]{0:T(128)}, u32[]{:S(2)}) copy-start(s32[8]{0:T(128)} %param.9) | copy-start | bytes 100
  1.8 90.0 %copy-start = (bf16[2,8,128,128]{3,2,1,0:T(8,128)(2,1)}, bf16[2,8,128,128]{3,2,1,0:T(8,128)(2,1)S(1)}, u32[]{:S(2)}) copy-start(bf16[2,8,128,128]{3,2,1,0:T(8,128)(2,1)S(1)} %maximum_bitcast_fusion.refs_11_) | copy-start | bytes 1572868
  1.8 14.9 %collective-permute-start.7 = (bf16[2,8,128,128]{3,2,1,0:T(8,128)(2,1)S(1)}, bf16[2,8,128,128]{3,2,1,0:T(8,128)(2,1)S(1)}, u32[]{:S(2)}, u32[]{:S(2)}) collective-permute-start(bf16[2,8,128,128]{3,2,1,0:T(8,128)(2,1)S(1)} %maximum_bitcast_fusion.refs_11_), channel_id=1, source_target_pairs={{0,1},{1,2},{2,3},{3,4},{4,5},{5,6},{6,7},{7,8},{8,9},{9,10},{10,1... | collective-permute-start | bytes 1572872 | tf_op jit(solution)/shard_map/ppermute | solution.py:141
  3.7 25.1 %collective-permute-start.6 = (bf16[2,8,128,128]{3,2,1,0:T(8,128)(2,1)S(1)}, bf16[2,8,128,128]{3,2,1,0:T(8,128)(2,1)S(1)}, u32[]{:S(2)}, u32[]{:S(2)}) collective-permute-start(bf16[2,8,128,128]{3,2,1,0:T(8,128)(2,1)S(1)} %maximum_bitcast_fusion.refs_11_), channel_id=1, source_target_pairs={{0,2},{1,3},{2,4},{3,5},{4,6},{5,7},{6,8},{7,9},{8,10},{9,11},{10,... | collective-permute-start | bytes 1572872 | tf_op jit(solution)/shard_map/ppermute | solution.py:141
  3.8 39.9 %collective-permute-start.5 = (bf16[2,8,128,128]{3,2,1,0:T(8,128)(2,1)S(1)}, bf16[2,8,128,128]{3,2,1,0:T(8,128)(2,1)S(1)}, u32[]{:S(2)}, u32[]{:S(2)}) collective-permute-start(bf16[2,8,128,128]{3,2,1,0:T(8,128)(2,1)S(1)} %maximum_bitcast_fusion.refs_11_), channel_id=1, source_target_pairs={{0,3},{1,4},{2,5},{3,6},{4,7},{5,8},{6,9},{7,10},{8,11},{9,12},{10... | collective-permute-start | bytes 1572872 | tf_op jit(solution)/shard_map/ppermute | solution.py:141
  6.4 49.3 %collective-permute-start.4 = (bf16[2,8,128,128]{3,2,1,0:T(8,128)(2,1)S(1)}, bf16[2,8,128,128]{3,2,1,0:T(8,128)(2,1)S(1)}, u32[]{:S(2)}, u32[]{:S(2)}) collective-permute-start(bf16[2,8,128,128]{3,2,1,0:T(8,128)(2,1)S(1)} %maximum_bitcast_fusion.refs_11_), channel_id=1, source_target_pairs={{0,4},{1,5},{2,6},{3,7},{4,8},{5,9},{6,10},{7,11},{8,12},{9,13},{1... | collective-permute-start | bytes 1572872 | tf_op jit(solution)/shard_map/ppermute | solution.py:141
  6.4 60.5 %collective-permute-start.3 = (bf16[2,8,128,128]{3,2,1,0:T(8,128)(2,1)S(1)}, bf16[2,8,128,128]{3,2,1,0:T(8,128)(2,1)S(1)}, u32[]{:S(2)}, u32[]{:S(2)}) collective-permute-start(bf16[2,8,128,128]{3,2,1,0:T(8,128)(2,1)S(1)} %maximum_bitcast_fusion.refs_11_), channel_id=1, source_target_pairs={{0,5},{1,6},{2,7},{3,8},{4,9},{5,10},{6,11},{7,12},{8,13},{9,14},{... | collective-permute-start | bytes 1572872 | tf_op jit(solution)/shard_map/ppermute | solution.py:141
  16.7 75.1 %copy-start.1 = (bf16[2,8,128,128]{3,2,1,0:T(8,128)(2,1)}, bf16[2,8,128,128]{3,2,1,0:T(8,128)(2,1)S(1)}, u32[]{:S(2)}) copy-start(bf16[2,8,128,128]{3,2,1,0:T(8,128)(2,1)S(1)} %collective-permute-done.7.refs_10_) | copy-start | bytes 1572868
  16.7 61.4 %collective-permute-start.2 = (bf16[2,8,128,128]{3,2,1,0:T(8,128)(2,1)S(1)}, bf16[2,8,128,128]{3,2,1,0:T(8,128)(2,1)}, u32[]{:S(2)}, u32[]{:S(2)}) collective-permute-start(bf16[2,8,128,128]{3,2,1,0:T(8,128)(2,1)S(1)} %maximum_bitcast_fusion.refs_11_), channel_id=1, source_target_pairs={{0,6},{1,7},{2,8},{3,9},{4,10},{5,11},{6,12},{7,13},{8,14},{9,15},... | collective-permute-start | bytes 1572872 | tf_op jit(solution)/shard_map/ppermute | solution.py:141
  28.7 63.1 %copy-start.2 = (bf16[2,8,128,128]{3,2,1,0:T(8,128)(2,1)}, bf16[2,8,128,128]{3,2,1,0:T(8,128)(2,1)S(1)}, u32[]{:S(2)}) copy-start(bf16[2,8,128,128]{3,2,1,0:T(8,128)(2,1)S(1)} %collective-permute-done.6.refs_9_) | copy-start | bytes 1572868
  28.7 57.2 %collective-permute-start.1 = (bf16[2,8,128,128]{3,2,1,0:T(8,128)(2,1)S(1)}, bf16[2,8,128,128]{3,2,1,0:T(8,128)(2,1)}, u32[]{:S(2)}, u32[]{:S(2)}) collective-permute-start(bf16[2,8,128,128]{3,2,1,0:T(8,128)(2,1)S(1)} %maximum_bitcast_fusion.refs_11_), channel_id=1, source_target_pairs={{0,7},{1,8},{2,9},{3,10},{4,11},{5,12},{6,13},{7,14},{8,15},{9,16}... | collective-permute-start | bytes 1572872 | tf_op jit(solution)/shard_map/ppermute | solution.py:141
  43.7 48.2 %copy-start.3 = (bf16[2,8,128,128]{3,2,1,0:T(8,128)(2,1)}, bf16[2,8,128,128]{3,2,1,0:T(8,128)(2,1)S(1)}, u32[]{:S(2)}) copy-start(bf16[2,8,128,128]{3,2,1,0:T(8,128)(2,1)S(1)} %collective-permute-done.5.refs_8_) | copy-start | bytes 1572868
  43.7 48.2 %collective-permute-start = (bf16[2,8,128,128]{3,2,1,0:T(8,128)(2,1)S(1)}, bf16[2,8,128,128]{3,2,1,0:T(8,128)(2,1)}, u32[]{:S(2)}, u32[]{:S(2)}) collective-permute-start(bf16[2,8,128,128]{3,2,1,0:T(8,128)(2,1)S(1)} %maximum_bitcast_fusion.refs_11_), channel_id=1, source_target_pairs={{0,8},{1,9},{2,10},{3,11},{4,12},{5,13},{6,14},{7,15},{8,16},{9,17... | collective-permute-start | bytes 1572872 | tf_op jit(solution)/shard_map/ppermute | solution.py:141
  55.7 36.2 %copy-start.4 = (bf16[2,8,128,128]{3,2,1,0:T(8,128)(2,1)}, bf16[2,8,128,128]{3,2,1,0:T(8,128)(2,1)S(1)}, u32[]{:S(2)}) copy-start(bf16[2,8,128,128]{3,2,1,0:T(8,128)(2,1)S(1)} %collective-permute-done.4.refs_7_) | copy-start | bytes 1572868
  66.9 25.0 %copy-start.5 = (bf16[2,8,128,128]{3,2,1,0:T(8,128)(2,1)}, bf16[2,8,128,128]{3,2,1,0:T(8,128)(2,1)S(1)}, u32[]{:S(2)}) copy-start(bf16[2,8,128,128]{3,2,1,0:T(8,128)(2,1)S(1)} %collective-permute-done.3.refs_6_) | copy-start | bytes 1572868
  153.7 14.5 %collective-permute-start.8 = (bf16[2,8,128,128]{3,2,1,0:T(8,128)(2,1)}, bf16[2,8,128,128]{3,2,1,0:T(8,128)(2,1)S(1)}, u32[]{:S(2)}, u32[]{:S(2)}) collective-permute-start(bf16[2,8,128,128]{3,2,1,0:T(8,128)(2,1)} %get-tuple-element.18), channel_id=1, source_target_pairs={{0,24},{1,25},{2,26},{3,27},{4,28},{5,29},{6,30},{7,31},{8,0},{9,1... | collective-permute-start | bytes 1572872 | tf_op jit(solution)/shard_map/ppermute | solution.py:141
  154.1 19.6 %collective-permute-start.9 = (bf16[2,8,128,128]{3,2,1,0:T(8,128)(2,1)}, bf16[2,8,128,128]{3,2,1,0:T(8,128)(2,1)S(1)}, u32[]{:S(2)}, u32[]{:S(2)}) collective-permute-start(bf16[2,8,128,128]{3,2,1,0:T(8,128)(2,1)} %get-tuple-element.19), channel_id=1, source_target_pairs={{0,25},{1,26},{2,27},{3,28},{4,29},{5,30},{6,31},{7,0},{8,1},{9,2}... | collective-permute-start | bytes 1572872 | tf_op jit(solution)/shard_map/ppermute | solution.py:141
  154.1 20.7 %collective-permute-start.10 = (bf16[2,8,128,128]{3,2,1,0:T(8,128)(2,1)}, bf16[2,8,128,128]{3,2,1,0:T(8,128)(2,1)S(1)}, u32[]{:S(2)}, u32[]{:S(2)}) collective-permute-start(bf16[2,8,128,128]{3,2,1,0:T(8,128)(2,1)} %get-tuple-element.20), channel_id=1, source_target_pairs={{0,26},{1,27},{2,28},{3,29},{4,30},{5,31},{6,0},{7,1},{8,2},{9,3},... | collective-permute-start | bytes 1572872 | tf_op jit(solution)/shard_map/ppermute | solution.py:141
  154.1 32.0 %collective-permute-start.11 = (bf16[2,8,128,128]{3,2,1,0:T(8,128)(2,1)}, bf16[2,8,128,128]{3,2,1,0:T(8,128)(2,1)S(1)}, u32[]{:S(2)}, u32[]{:S(2)}) collective-permute-start(bf16[2,8,128,128]{3,2,1,0:T(8,128)(2,1)} %get-tuple-element.21), channel_id=1, source_target_pairs={{0,27},{1,28},{2,29},{3,30},{4,31},{5,0},{6,1},{7,2},{8,3},{9,4},{... | collective-permute-start | bytes 1572872 | tf_op jit(solution)/shard_map/ppermute | solution.py:141
  154.1 43.2 %collective-permute-start.12 = (bf16[2,8,128,128]{3,2,1,0:T(8,128)(2,1)}, bf16[2,8,128,128]{3,2,1,0:T(8,128)(2,1)S(1)}, u32[]{:S(2)}, u32[]{:S(2)}) collective-permute-start(bf16[2,8,128,128]{3,2,1,0:T(8,128)(2,1)} %get-tuple-element.22), channel_id=1, source_target_pairs={{0,28},{1,29},{2,30},{3,31},{4,0},{5,1},{6,2},{7,3},{8,4},{9,5},{1... | collective-permute-start | bytes 1572872 | tf_op jit(solution)/shard_map/ppermute | solution.py:141
  168.2 29.1 %collective-permute-start.13 = (bf16[2,8,128,128]{3,2,1,0:T(8,128)(2,1)}, bf16[2,8,128,128]{3,2,1,0:T(8,128)(2,1)S(1)}, u32[]{:S(2)}, u32[]{:S(2)}) collective-permute-start(bf16[2,8,128,128]{3,2,1,0:T(8,128)(2,1)} %get-tuple-element.23), channel_id=1, source_target_pairs={{0,29},{1,30},{2,31},{3,0},{4,1},{5,2},{6,3},{7,4},{8,5},{9,6},{10... | collective-permute-start | bytes 1572872 | tf_op jit(solution)/shard_map/ppermute | solution.py:141
  173.7 23.6 %collective-permute-start.14 = (bf16[2,8,128,128]{3,2,1,0:T(8,128)(2,1)}, bf16[2,8,128,128]{3,2,1,0:T(8,128)(2,1)S(1)}, u32[]{:S(2)}, u32[]{:S(2)}) collective-permute-start(bf16[2,8,128,128]{3,2,1,0:T(8,128)(2,1)} %get-tuple-element.24), channel_id=1, source_target_pairs={{0,30},{1,31},{2,0},{3,1},{4,2},{5,3},{6,4},{7,5},{8,6},{9,7},{10,... | collective-permute-start | bytes 1572872 | tf_op jit(solution)/shard_map/ppermute | solution.py:141
  174.8 28.8 %collective-permute-start.15 = (bf16[2,8,128,128]{3,2,1,0:T(8,128)(2,1)}, bf16[2,8,128,128]{3,2,1,0:T(8,128)(2,1)S(1)}, u32[]{:S(2)}, u32[]{:S(2)}) collective-permute-start(bf16[2,8,128,128]{3,2,1,0:T(8,128)(2,1)} %get-tuple-element.25), channel_id=1, source_target_pairs={{0,31},{1,0},{2,1},{3,2},{4,3},{5,4},{6,5},{7,6},{8,7},{9,8},{10,9... | collective-permute-start | bytes 1572872 | tf_op jit(solution)/shard_map/ppermute | solution.py:141

commit v2 on v1

v2 whole, which is shorter than its diff:
```python
import functools

import jax
import jax.numpy as jnp
from jax import lax
from jax.experimental import pallas as pl
from jax.experimental.pallas import tpu as pltpu
from jax.sharding import PartitionSpec as P

MOST = 1024
AXES = ("ctx", "head")
MASKED = -1e30


def document_starts(doc_lengths, positions):
    doc_ends = jnp.cumsum(doc_lengths)
    earlier = jnp.where(doc_ends[None, :] <= positions[:, None], doc_lengths[None, :], 0)
    return jnp.sum(earlier, axis=1)


def nt(left, right):
    return lax.dot_general(
        left, right, (((1,), (1,)), ((), ())), preferred_element_type=jnp.float32
    )


def nn(left, right):
    return jnp.dot(left, right, preferred_element_type=jnp.float32)


def attention_kernel(
    steps, rows, ctx_size, head_size, ahead, behind, score_scale,
    bounds_ref, q_ref, do_ref, own_ref, o_ref, dq_ref, dkv_ref,
    window, leaving, landed, own_part, bias, k_s, v_s, kt_s, vt_s, dk_s, dv_s,
    kv_send, kv_recv, d_send, d_recv,
):
    tokens, width, size_head = q_ref.shape
    span = (steps + 1) * tokens
    total_rows = tokens * width
    devices = ctx_size * head_size
    g = pl.program_id(0)
    kv_count = pl.num_programs(0)
    me = lax.axis_index("ctx") * head_size + lax.axis_index("head")

    def peer(distance):
        other = lax.rem(me + distance + devices, devices)
        return (other // head_size, lax.rem(other, head_size))

    def send_block(head, s):
        return pltpu.make_async_remote_copy(
            src_ref=own_ref.at[head],
            dst_ref=window.at[head, steps - s],
            send_sem=kv_send.at[head],
            recv_sem=kv_recv.at[head],
            device_id=peer(s),
            device_id_type=pl.DeviceIdType.MESH,
        )

    def send_part(head, s):
        return pltpu.make_async_remote_copy(
            src_ref=leaving.at[head, steps - s],
            dst_ref=landed.at[head, steps - s],
            send_sem=d_send.at[head],
            recv_sem=d_recv.at[head],
            device_id=peer(-s),
            device_id_type=pl.DeviceIdType.MESH,
        )

    def send_blocks(head):
        @pl.loop(0, steps)
        def _(i):
            send_block(head, steps - i).start()

    def send_parts(head):
        @pl.loop(0, steps)
        def _(i):
            send_part(head, steps - i).start()

    def wait_all(ref, sem):
        pltpu.make_async_copy(ref, ref, sem).wait()

    def finish(head):
        wait_all(landed.at[head], d_recv.at[head])
        for which in range(2):
            total = own_part[head, which]
            for i in range(steps):
                total = total + landed[head, i, which].astype(jnp.float32)
            dkv_ref[head, which] = total.astype(dkv_ref.dtype)

    @pl.when(g == 0)
    def _():
        barrier = pltpu.get_barrier_semaphore()

        @pl.loop(1, steps + 1)
        def _(s):
            for d in (s, -s):
                pl.semaphore_signal(
                    barrier, inc=1, device_id=peer(d), device_id_type=pl.DeviceIdType.MESH
                )

        pl.semaphore_wait(barrier, 2 * steps)

        @pl.loop(0, ahead)
        def _(head):
            send_blocks(head)

        key_at = lax.broadcasted_iota(jnp.int32, (span, total_rows), 0)
        allowed = (key_at >= bounds_ref[0:1, :]) & (key_at <= bounds_ref[1:2, :])
        bias[...] = jnp.where(allowed, 0.0, MASKED)

    @pl.when(g + ahead < kv_count)
    def _():
        send_blocks(g + ahead)

    @pl.when(g > 0)
    def _():
        send_parts(g - 1)

    wait_all(window.at[g], kv_recv.at[g])
    for i in range(steps + 1):
        at = pl.ds(i * tokens, tokens)
        k_s[at, :] = window[g, i, 0] if i < steps else own_ref[g, 0]
        v_s[at, :] = window[g, i, 1] if i < steps else own_ref[g, 1]
    kt_s[...] = k_s[...].T
    vt_s[...] = v_s[...].T
    dk_s[...] = jnp.zeros_like(dk_s)
    dv_s[...] = jnp.zeros_like(dv_s)
    part = rows // width

    @pl.loop(0, total_rows // rows)
    def _(c):
        toks = pl.ds(pl.multiple_of(c * part, part), part)
        lanes = pl.ds(pl.multiple_of(c * rows, rows), rows)
        q = q_ref[toks].reshape(rows, size_head)
        do = do_ref[toks].reshape(rows, size_head)
        x = nt(k_s[...], q) + bias[:, lanes]
        top = jnp.max(x, axis=0, keepdims=True)
        e = jnp.exp((x - top) * score_scale)
        inv = 1.0 / jnp.sum(e, axis=0, keepdims=True)
        p = e * inv
        w = p.astype(jnp.bfloat16)
        ot = nn(vt_s[...], w).astype(jnp.bfloat16)
        dot_f = do.T.astype(jnp.float32)
        delta = jnp.sum(dot_f * ot.astype(jnp.float32), axis=0, keepdims=True)
        o_ref[toks] = ot.T.reshape(part, width, size_head)
        dp = nt(v_s[...], do)
        ds = (p * (dp - delta)).astype(jnp.bfloat16)
        dv_s[...] += nn(w, do)
        dk_s[...] += nn(ds, q)
        dqt = (nn(kt_s[...], ds) * score_scale).astype(jnp.bfloat16)
        dq_ref[toks] = dqt.T.reshape(part, width, size_head)

    for i in range(steps):
        at = pl.ds(i * tokens, tokens)
        leaving[g, i, 0] = (dk_s[at, :] * score_scale).astype(leaving.dtype)
        leaving[g, i, 1] = dv_s[at, :].astype(leaving.dtype)
    at = pl.ds(steps * tokens, tokens)
    own_part[g, 0] = dk_s[at, :] * score_scale
    own_part[g, 1] = dv_s[at, :]

    @pl.when(g >= behind)
    def _():
        finish(g - behind)

    @pl.when(g == kv_count - 1)
    def _():
        send_parts(g)

        @pl.loop(0, behind)
        def _(i):
            finish(g - behind + 1 + i)

        @pl.loop(0, kv_count)
        def _(head):
            wait_all(window.at[head], kv_send.at[head])
            wait_all(leaving.at[head], d_send.at[head])


def attention(queries, output_gradient, own, bounds, steps, score_scale):
    tokens, heads, size_head = queries.shape
    kv_count = own.shape[0]
    width = heads // kv_count
    span = (steps + 1) * tokens
    total_rows = tokens * width
    rows = min(256, total_rows)
    q4 = queries.reshape(tokens, kv_count, width, size_head)
    do4 = output_gradient.reshape(tokens, kv_count, width, size_head)
    row_spec = pl.BlockSpec((tokens, None, width, size_head), lambda g: (0, g, 0, 0))
    row_shape = jax.ShapeDtypeStruct(q4.shape, jnp.bfloat16)
    full = pl.BlockSpec(own.shape, lambda g: (0, 0, 0, 0))
    slots = (kv_count, steps) + own.shape[1:]
    outs = pl.pallas_call(
        functools.partial(
            attention_kernel,
            steps,
            rows,
            lax.axis_size("ctx"),
            lax.axis_size("head"),
            min(3, kv_count),
            min(3, kv_count - 1),
            score_scale,
        ),
        grid=(kv_count,),
        in_specs=[pl.BlockSpec((2, total_rows), lambda g: (0, 0)), row_spec, row_spec, full],
        out_specs=[row_spec, row_spec, full],
        out_shape=[row_shape, row_shape, jax.ShapeDtypeStruct(own.shape, jnp.bfloat16)],
        scratch_shapes=[
            pltpu.VMEM(slots, jnp.bfloat16),
            pltpu.VMEM(slots, jnp.bfloat16),
            pltpu.VMEM(slots, jnp.bfloat16),
            pltpu.VMEM(own.shape, jnp.float32),
            pltpu.VMEM((span, total_rows), jnp.float32),
            pltpu.VMEM((span, size_head), jnp.bfloat16),
            pltpu.VMEM((span, size_head), jnp.bfloat16),
            pltpu.VMEM((size_head, span), jnp.bfloat16),
            pltpu.VMEM((size_head, span), jnp.bfloat16),
            pltpu.VMEM((span, size_head), jnp.float32),
            pltpu.VMEM((span, size_head), jnp.float32),
            pltpu.SemaphoreType.DMA((kv_count,)),
            pltpu.SemaphoreType.DMA((kv_count,)),
            pltpu.SemaphoreType.DMA((kv_count,)),
            pltpu.SemaphoreType.DMA((kv_count,)),
        ],
        compiler_params=pltpu.CompilerParams(
            dimension_semantics=("arbitrary",),
            vmem_limit_bytes=60 << 20,
            collective_id=0,
            has_side_effects=True,
        ),
        name="attention",
    )(bounds, q4, do4, own)
    return outs[0].reshape(queries.shape), outs[1].reshape(queries.shape), outs[2]


def body(queries, key_heads, head_values, output_gradient, doc_lengths):
    tokens, heads, size_head = queries.shape
    width = heads // key_heads.shape[1]
    steps = (MOST + tokens - 2) // tokens
    base = (lax.axis_index("ctx") * lax.axis_size("head") + lax.axis_index("head")) * tokens
    query_pos = base + jnp.arange(tokens, dtype=jnp.int32)
    query_start = document_starts(doc_lengths, query_pos)
    window_base = base - steps * tokens
    bounds = jnp.stack([query_start, query_pos], 0) - window_base
    bounds = jnp.repeat(bounds, width, axis=1)
    own = jnp.transpose(jnp.stack([key_heads, head_values], 0), (2, 0, 1, 3))
    attended, grad_query, total = attention(
        queries, output_gradient, own, bounds, steps, size_head ** (-0.5)
    )
    total = jnp.transpose(total, (1, 2, 0, 3))
    return attended, grad_query, total[0], total[1]


def solution(mesh):
    whole = P(AXES, None, None)
    return jax.shard_map(
        body,
        mesh=mesh,
        in_specs=(whole, whole, whole, whole, P()),
        out_specs=(whole, whole, whole, whole),
        check_vma=False,
    )
```

time: 210 us -> 132 us (0.63)
  waiting for transfers between devices: 123 us -> 0 us
  Pallas kernels: 61.8 us -> 118 us
  starting transfers between devices: 16 us -> 0 us
  local copies, waits for them, and re-layouts: 3.75 us -> 8.57 us
    ppermute x16 -> x0, waiting for transfers between devices: 123 us -> none  [moved(): return lax.ppermute(block, AXES, route)]
    pallas_call x1, Pallas kernels: 61.8 us -> 118 us  [attention(): pl.pallas_call(functools.partial(attention_kernel, steps, rows, lax.axis_...]
    ppermute x16 -> x0, starting transfers between devices: 16 us -> none  [moved(): return lax.ppermute(block, AXES, route)]
    unnamed x16 -> x8, local copies, waits for them, and re-layouts: 1.78 us -> 5.42 us
  transfers between devices with their start and end apart: 16 -> 0, of which waited for: 14 -> 0; matrix products, arithmetic and copies ran while one was open for 1% -> 0% of each run, Pallas kernels for 0% -> 0%
where the time goes in v2:
time: 132 us; the launch traced here: 130 us
  Pallas kernels  118 us (89%)
  local copies, waits for them, and re-layouts  8.57 us (6%)
  other arithmetic  2.43 us (2%)
    pallas_call x1, Pallas kernels, attention(): pl.pallas_call(functools.partial(attention_kernel, steps, rows, lax.axis_...  118 us
    unnamed x8, local copies, waits for them, and re-layouts  5.42 us

profile of v2, /device:TPU:23, one launch (start us, length us, event | category | flops | bytes accessed | tf_op | source)
XLA Modules:
  0.0 129.9 jit_solution(9998490000486278399)
XLA Ops:
  0.6 0.8 reduce-window.8
  1.5 0.7 select_reduce_fusion
  2.2 0.1 broadcast_in_dim.20
  2.3 0.7 reshape.61.bounds_ref
  3.0 1.1 copy_bitcast_fusion
  4.2 0.8 maximum_bitcast_fusion.own_ref
  5.0 118.2 %attention.1 = (bf16[128,8,8,128]{3,2,1,0:T(8,128)(2,1)}, bf16[128,8,8,128]{3,2,1,0:T(8,128)(2,1)}, bf16[8,2,128,128]{3,2,1,0:T(8,128)(2,1)}) custom-call(s32[2,1024]{1,0:T(2,128)} %reshape.61.bounds_ref, bf16[128,8,8,128]{3,2,1,0:T(8,128)(2,1)} %bitcast.18, bf16[128,8,8,128]{3,2,1,0:T(8,128)(2,1)} %bitcast.19, ...), custom_call_target="tpu_custom_call" | custom-call | tf_op jit(solution)/shard_map/attention/pallas_call | solution.py:192
  123.3 0.0 copy-start.1
  123.3 1.2 slice_bitcast_fusion
  124.5 0.9 copy.20
  125.4 0.9 copy.19
  126.2 0.0 copy-done.1
  126.3 0.0 copy-start
  126.3 1.3 %copy.25 = bf16[128,64,128]{2,1,0:T(8,128)(2,1)} copy(bf16[128,64,128]{2,1,0:T(8,128)(2,1)S(1)} %bitcast.21) | data formatting | bytes 4194304
  127.6 1.0 copy-done
  128.6 1.3 %copy.26 = bf16[128,64,128]{2,1,0:T(8,128)(2,1)} copy(bf16[128,64,128]{2,1,0:T(8,128)(2,1)S(1)} %bitcast.20) | data formatting | bytes 4194304
  (3 shorter events, 0.0 us)
Async XLA Ops:
  123.3 3.0 %copy-start.1 = (bf16[128,8,8,128]{3,2,1,0:T(8,128)(2,1)S(1)}, bf16[128,8,8,128]{3,2,1,0:T(8,128)(2,1)}, u32[]{:S(2)}) copy-start(bf16[128,8,8,128]{3,2,1,0:T(8,128)(2,1)} %get-tuple-element.7) | copy-start | bytes 6291460
  126.3 2.3 %copy-start = (bf16[128,8,8,128]{3,2,1,0:T(8,128)(2,1)S(1)}, bf16[128,8,8,128]{3,2,1,0:T(8,128)(2,1)}, u32[]{:S(2)}) copy-start(bf16[128,8,8,128]{3,2,1,0:T(8,128)(2,1)} %get-tuple-element.8) | copy-start | bytes 6291460

commit v3 on v2

v3 whole, which is shorter than its diff:
```python
import functools

import jax
import jax.numpy as jnp
from jax import lax
from jax.experimental import pallas as pl
from jax.experimental.pallas import tpu as pltpu
from jax.sharding import PartitionSpec as P

MOST = 1024
AXES = ("ctx", "head")
MASKED = -1e30


def document_starts(doc_lengths, positions):
    doc_ends = jnp.cumsum(doc_lengths)
    earlier = jnp.where(doc_ends[None, :] <= positions[:, None], doc_lengths[None, :], 0)
    return jnp.sum(earlier, axis=1)


def nt(left, right):
    return lax.dot_general(
        left, right, (((1,), (1,)), ((), ())), preferred_element_type=jnp.float32
    )


def nn(left, right):
    return jnp.dot(left, right, preferred_element_type=jnp.float32)


def attention_kernel(
    steps, rows, ctx_size, head_size, ahead, behind, score_scale,
    bounds_ref, q_ref, do_ref, own_ref, o_ref, dq_ref, dkv_ref,
    window, leaving, landed, own_part, bias, q_s, do_s, o_s, dq_s,
    k_s, v_s, kt_s, vt_s, dk_s, dv_s,
    kv_send, kv_recv, d_send, d_recv, row_here, row_send, row_recv, out_here, out_send, out_recv,
):
    local_heads, slots = window.shape[:2]
    tokens, width, size_head = q_s.shape[2:]
    span = (steps + 1) * tokens
    total_rows = tokens * width
    part = rows // width
    g = pl.program_id(0)
    ctx = lax.axis_index("ctx")
    core = lax.rem(ctx, 2)
    me = ctx * head_size + lax.axis_index("head")
    base = me - core * head_size
    devices = ctx_size * head_size
    mesh_ids = pl.DeviceIdType.MESH
    sibling = (ctx + 1 - 2 * core, lax.axis_index("head"))

    def at_device(flat):
        return (flat // head_size, lax.rem(flat, head_size))

    def each_target(visit):
        @pl.loop(0, slots)
        def _(i):
            chip = me - head_size + i

            @pl.when((chip >= 0) & (chip < devices))
            def _():
                @pl.when(lax.rem(chip // head_size, 2) == 0)
                def _():
                    for side in range(2):
                        target = chip + side * head_size

                        @pl.when(target != me)
                        def _():
                            visit(i, side, target)

    def each_source(visit):
        @pl.loop(0, slots)
        def _(j):
            source = base - steps + j

            @pl.when((source >= 0) & (source != me))
            def _():
                visit(j, source)

    def block_copy(k, i, side, target):
        slot = slots - 1 - i
        return pltpu.make_async_remote_copy(
            src_ref=own_ref.at[side * local_heads + k],
            dst_ref=window.at[k, slot],
            send_sem=kv_send.at[k],
            recv_sem=kv_recv.at[k, slot],
            device_id=at_device(target),
            device_id_type=mesh_ids,
        )

    def part_copy(k, j, source):
        head = core * local_heads + k
        return pltpu.make_async_remote_copy(
            src_ref=leaving.at[k, j],
            dst_ref=landed.at[head, slots - 1 - j],
            send_sem=d_send.at[k],
            recv_sem=d_recv.at[head, slots - 1 - j],
            device_id=at_device(source),
            device_id_type=mesh_ids,
        )

    def row_copies(k, n):
        src, dst = ((q_ref, q_s), (do_ref, do_s))[n]
        here = pltpu.make_async_copy(
            src.at[:, core * local_heads + k], dst.at[k, core], row_here.at[k, n]
        )
        away = pltpu.make_async_remote_copy(
            src_ref=src.at[:, (1 - core) * local_heads + k],
            dst_ref=dst.at[k, core],
            send_sem=row_send.at[k, n],
            recv_sem=row_recv.at[k, n],
            device_id=sibling,
            device_id_type=mesh_ids,
        )
        return here, away

    def out_copies(k, n):
        src, dst = ((o_s, o_ref), (dq_s, dq_ref))[n]
        head = core * local_heads + k
        here = pltpu.make_async_copy(src.at[k, core], dst.at[:, head], out_here.at[k, n])
        away = pltpu.make_async_remote_copy(
            src_ref=src.at[k, 1 - core],
            dst_ref=dst.at[:, head],
            send_sem=out_send.at[k, n],
            recv_sem=out_recv.at[k, n],
            device_id=sibling,
            device_id_type=mesh_ids,
        )
        return here, away

    def fetch(k):
        for n in range(2):
            here, away = row_copies(k, n)
            away.start()
            here.start()
        each_target(lambda i, side, target: block_copy(k, i, side, target).start())

    def give(k):
        each_source(lambda j, source: part_copy(k, j, source).start())
        for n in range(2):
            here, away = out_copies(k, n)
            away.start()
            here.start()

    def finish(k):
        def add(i, side, target):
            head = side * local_heads + k
            pltpu.make_async_copy(landed.at[head, i], landed.at[head, i], d_recv.at[head, i]).wait()
            own_part[head] += landed[head, i].astype(jnp.float32)

        each_target(add)
        for side in range(2):
            head = side * local_heads + k
            dkv_ref[head] = own_part[head].astype(dkv_ref.dtype)

    @pl.when(g == 0)
    def _():
        barrier = pltpu.get_barrier_semaphore()

        def greet(flat):
            pl.semaphore_signal(
                barrier, inc=1, device_id=at_device(flat), device_id_type=mesh_ids
            )

        each_target(lambda i, side, target: greet(target))
        each_source(lambda j, source: greet(source))
        greeted = jnp.int32(0)
        for i in range(slots):
            chip = me - head_size + i
            is_chip = (chip >= 0) & (chip < devices)
            is_chip = is_chip & (lax.rem(chip // head_size, 2) == 0)
            for side in range(2):
                met = is_chip & (chip + side * head_size != me)
                greeted = greeted + jnp.where(met, 1, 0)
            source = base - steps + i
            greeted = greeted + jnp.where((source >= 0) & (source != me), 1, 0)
        pl.semaphore_wait(barrier, greeted)

        @pl.loop(0, ahead)
        def _(k):
            fetch(k)

        own_part[...] = jnp.zeros_like(own_part)
        key_at = lax.broadcasted_iota(jnp.int32, (span, total_rows), 0)
        for b in range(2):
            low, high = bounds_ref[2 * b : 2 * b + 1, :], bounds_ref[2 * b + 1 : 2 * b + 2, :]
            bias[b] = jnp.where((key_at >= low) & (key_at <= high), 0.0, MASKED)

    @pl.when((g > 0) & (g + ahead - 1 < local_heads))
    def _():
        fetch(g + ahead - 1)

    @pl.when(g > 0)
    def _():
        give(g - 1)

    for n in range(2):
        here, away = row_copies(g, n)
        here.wait()
        away.wait_recv()

    @pl.loop(0, slots)
    def _(j):
        source = base - steps + j
        at = pl.ds(pl.multiple_of(j * tokens, tokens), tokens)

        @pl.when(source < 0)
        def _():
            k_s[at, :] = jnp.zeros((tokens, size_head), k_s.dtype)
            v_s[at, :] = jnp.zeros((tokens, size_head), v_s.dtype)

        @pl.when(source == me)
        def _():
            k_s[at, :] = own_ref[core * local_heads + g, 0]
            v_s[at, :] = own_ref[core * local_heads + g, 1]

        @pl.when((source >= 0) & (source != me))
        def _():
            pltpu.make_async_copy(window.at[g, j], window.at[g, j], kv_recv.at[g, j]).wait()
            k_s[at, :] = window[g, j, 0]
            v_s[at, :] = window[g, j, 1]

    kt_s[...] = k_s[...].T
    vt_s[...] = v_s[...].T
    dk_s[...] = jnp.zeros_like(dk_s)
    dv_s[...] = jnp.zeros_like(dv_s)

    for b in range(2):
        near = pl.ds(b * head_size * tokens, span)

        @pl.loop(0, total_rows // rows)
        def _(c):
            toks = pl.ds(pl.multiple_of(c * part, part), part)
            lanes = pl.ds(pl.multiple_of(c * rows, rows), rows)
            q = q_s[g, b, toks].reshape(rows, size_head)
            do = do_s[g, b, toks].reshape(rows, size_head)
            x = nt(k_s[near, :], q) + bias[b, :, lanes]
            top = jnp.max(x, axis=0, keepdims=True)
            e = jnp.exp((x - top) * score_scale)
            inv = 1.0 / jnp.sum(e, axis=0, keepdims=True)
            p = e * inv
            w = p.astype(jnp.bfloat16)
            ot = nn(vt_s[:, near], w).astype(jnp.bfloat16)
            dot_f = do.T.astype(jnp.float32)
            delta = jnp.sum(dot_f * ot.astype(jnp.float32), axis=0, keepdims=True)
            o_s[g, b, toks] = ot.T.reshape(part, width, size_head)
            dp = nt(v_s[near, :], do)
            ds = (p * (dp - delta)).astype(jnp.bfloat16)
            dv_s[near, :] += nn(w, do)
            dk_s[near, :] += nn(ds, q)
            dqt = (nn(kt_s[:, near], ds) * score_scale).astype(jnp.bfloat16)
            dq_s[g, b, toks] = dqt.T.reshape(part, width, size_head)

    for j in range(slots):
        at = pl.ds(j * tokens, tokens)
        leaving[g, j, 0] = (dk_s[at, :] * score_scale).astype(leaving.dtype)
        leaving[g, j, 1] = dv_s[at, :].astype(leaving.dtype)
    at = pl.ds(pl.multiple_of((steps + core * head_size) * tokens, tokens), tokens)
    own_part[core * local_heads + g, 0] += dk_s[at, :] * score_scale
    own_part[core * local_heads + g, 1] += dv_s[at, :]

    @pl.when(g >= behind)
    def _():
        finish(g - behind)

    @pl.when(g == local_heads - 1)
    def _():
        give(g)

        @pl.loop(0, behind)
        def _(i):
            finish(g - behind + 1 + i)

        @pl.loop(0, local_heads)
        def _(k):
            each_target(lambda i, side, target: block_copy(k, i, side, target).wait_send())
            each_source(lambda j, source: part_copy(k, j, source).wait_send())
            for n in range(2):
                row_copies(k, n)[1].wait_send()
                here, away = out_copies(k, n)
                here.wait()
                away.wait()


def attention(queries, output_gradient, own, bounds, steps, score_scale):
    tokens, heads, size_head = queries.shape
    kv_count = own.shape[0]
    width = heads // kv_count
    local_heads = kv_count // 2
    span = (steps + 1) * tokens
    slots = steps + 1 + lax.axis_size("head")
    reach = slots * tokens
    total_rows = tokens * width
    rows = min(256, total_rows)
    q4 = queries.reshape(tokens, kv_count, width, size_head)
    do4 = output_gradient.reshape(tokens, kv_count, width, size_head)
    anywhere = pl.BlockSpec(memory_space=pl.ANY)
    row_shape = jax.ShapeDtypeStruct(q4.shape, jnp.bfloat16)
    full = pl.BlockSpec(own.shape, lambda g: (0, 0, 0, 0))
    row_buffer = pltpu.VMEM((local_heads, 2, tokens, width, size_head), jnp.bfloat16)
    pair = pltpu.SemaphoreType.DMA((local_heads, 2))
    outs = pl.pallas_call(
        functools.partial(
            attention_kernel,
            steps,
            rows,
            lax.axis_size("ctx"),
            lax.axis_size("head"),
            min(2, local_heads),
            min(2, local_heads - 1),
            score_scale,
        ),
        grid=(local_heads,),
        in_specs=[pl.BlockSpec((4, total_rows), lambda g: (0, 0)), anywhere, anywhere, full],
        out_specs=[anywhere, anywhere, full],
        out_shape=[row_shape, row_shape, jax.ShapeDtypeStruct(own.shape, jnp.bfloat16)],
        scratch_shapes=[
            pltpu.VMEM((local_heads, slots) + own.shape[1:], jnp.bfloat16),
            pltpu.VMEM((local_heads, slots) + own.shape[1:], jnp.bfloat16),
            pltpu.VMEM((kv_count, slots) + own.shape[1:], jnp.bfloat16),
            pltpu.VMEM(own.shape, jnp.float32),
            pltpu.VMEM((2, span, total_rows), jnp.float32),
            row_buffer,
            row_buffer,
            row_buffer,
            row_buffer,
            pltpu.VMEM((reach, size_head), jnp.bfloat16),
            pltpu.VMEM((reach, size_head), jnp.bfloat16),
            pltpu.VMEM((size_head, reach), jnp.bfloat16),
            pltpu.VMEM((size_head, reach), jnp.bfloat16),
            pltpu.VMEM((reach, size_head), jnp.float32),
            pltpu.VMEM((reach, size_head), jnp.float32),
            pltpu.SemaphoreType.DMA((local_heads,)),
            pltpu.SemaphoreType.DMA((local_heads, slots)),
            pltpu.SemaphoreType.DMA((local_heads,)),
            pltpu.SemaphoreType.DMA((kv_count, slots)),
            pair,
            pair,
            pair,
            pair,
            pair,
            pair,
        ],
        compiler_params=pltpu.CompilerParams(
            dimension_semantics=("arbitrary",),
            vmem_limit_bytes=60 << 20,
            collective_id=0,
            has_side_effects=True,
        ),
        name="attention",
    )(bounds, q4, do4, own)
    return outs[0].reshape(queries.shape), outs[1].reshape(queries.shape), outs[2]


def body(queries, key_heads, head_values, output_gradient, doc_lengths):
    tokens, heads, size_head = queries.shape
    width = heads // key_heads.shape[1]
    steps = (MOST + tokens - 2) // tokens
    ctx, head_size = lax.axis_index("ctx"), lax.axis_size("head")
    chip = (ctx - ctx % 2) * head_size + lax.axis_index("head")
    within = jnp.arange(tokens, dtype=jnp.int32)
    bounds = []
    for b in range(2):
        base = (chip + b * head_size) * tokens
        window_base = base - steps * tokens
        query_pos = base + within
        bounds += [document_starts(doc_lengths, query_pos) - window_base, query_pos - window_base]
    bounds = jnp.repeat(jnp.stack(bounds, 0), width, axis=1)
    own = jnp.transpose(jnp.stack([key_heads, head_values], 0), (2, 0, 1, 3))
    attended, grad_query, total = attention(
        queries, output_gradient, own, bounds, steps, size_head ** (-0.5)
    )
    total = jnp.transpose(total, (1, 2, 0, 3))
    return attended, grad_query, total[0], total[1]


def solution(mesh):
    whole = P(AXES, None, None)
    return jax.shard_map(
        body,
        mesh=mesh,
        in_specs=(whole, whole, whole, whole, P()),
        out_specs=(whole, whole, whole, whole),
        check_vma=False,
    )
```

time: 132 us -> 106 us (0.80); the launches traced: 130 us -> 105 us
  Pallas kernels: 118 us -> 93.6 us
    pallas_call x1, Pallas kernels: 118 us -> 93.6 us  [attention(): pl.pallas_call(functools.partial(attention_kernel, steps, rows, lax.axis_...]
where the time goes in v3:
time: 106 us; the launch traced here: 105 us
  Pallas kernels  93.6 us (88%)
  local copies, waits for them, and re-layouts  8.65 us (8%)
  other arithmetic  2.44 us (2%)
    pallas_call x1, Pallas kernels, attention(): pl.pallas_call(functools.partial(attention_kernel, steps, rows, lax.axis_...  93.6 us
    unnamed x8, local copies, waits for them, and re-layouts  5.42 us

profile of v3, /device:TPU:23, one launch (start us, length us, event | category | flops | bytes accessed | tf_op | source)
XLA Modules:
  0.0 105.4 jit_solution(3384190562446696494)
XLA Ops:
  0.6 0.8 reduce-window.8
  1.5 0.7 select_reduce_fusion.1
  2.3 0.1 broadcast_in_dim.27
  2.4 0.8 reshape.96.bounds_ref
  3.2 1.1 %copy_bitcast_fusion = (bf16[1,128,8,128]{3,1,0,2:T(8,128)(2,1)S(1)}, bf16[1,128,8,128]{3,1,0,2:T(8,128)(2,1)S(1)}) fusion(bf16[128,8,128]{2,1,0:T(8,128)(2,1)} %param.7, bf16[128,8,128]{2,1,0:T(8,128)(2,1)} %param.6), kind=kLoop, calls=%fused_computation.3 | loop fusion | bytes 1048576 | tf_op jit(solution)/shard_map/stack | solution.py:369
  4.3 0.8 maximum_bitcast_fusion.own_ref
  5.1 93.6 %attention.1 = (bf16[128,8,8,128]{3,2,1,0:T(8,128)(2,1)}, bf16[128,8,8,128]{3,2,1,0:T(8,128)(2,1)}, bf16[8,2,128,128]{3,2,1,0:T(8,128)(2,1)}) custom-call(s32[4,1024]{1,0:T(4,128)} %reshape.96.bounds_ref, bf16[128,8,8,128]{3,2,1,0:T(8,128)(2,1)} %bitcast.21, bf16[128,8,8,128]{3,2,1,0:T(8,128)(2,1)} %bitcast.22, ...), custom_call_target="tpu_custom_call" | custom-call | tf_op jit(solution)/shard_map/attention/pallas_call | solution.py:302
  98.7 0.0 copy-start.1
  98.7 1.2 %slice_bitcast_fusion = (bf16[128,8,128]{2,0,1:T(8,128)(2,1)S(1)}, bf16[128,8,128]{2,0,1:T(8,128)(2,1)S(1)}) fusion(bf16[2,128,8,128]{3,1,0,2:T(8,128)(2,1)} %bitcast.25), kind=kLoop, calls=%fused_computation.1 | loop fusion | bytes 1048576 | tf_op jit(solution)/shard_map/squeeze | solution.py:374
  99.9 0.9 copy.20
  100.8 0.9 copy.19
  101.7 0.0 copy-done.1
  101.7 0.0 copy-start
  101.7 1.3 %copy.25 = bf16[128,64,128]{2,1,0:T(8,128)(2,1)} copy(bf16[128,64,128]{2,1,0:T(8,128)(2,1)S(1)} %bitcast.24) | data formatting | bytes 4194304
  103.0 1.0 copy-done
  104.0 1.3 %copy.26 = bf16[128,64,128]{2,1,0:T(8,128)(2,1)} copy(bf16[128,64,128]{2,1,0:T(8,128)(2,1)S(1)} %bitcast.23) | data formatting | bytes 4194304
  (5 shorter events, 0.0 us)
Async XLA Ops:
  98.7 3.0 %copy-start.1 = (bf16[128,8,8,128]{3,2,1,0:T(8,128)(2,1)S(1)}, bf16[128,8,8,128]{3,2,1,0:T(8,128)(2,1)}, u32[]{:S(2)}) copy-start(bf16[128,8,8,128]{3,2,1,0:T(8,128)(2,1)} %get-tuple-element.7) | copy-start | bytes 6291460
  101.7 2.3 %copy-start = (bf16[128,8,8,128]{3,2,1,0:T(8,128)(2,1)S(1)}, bf16[128,8,8,128]{3,2,1,0:T(8,128)(2,1)}, u32[]{:S(2)}) copy-start(bf16[128,8,8,128]{3,2,1,0:T(8,128)(2,1)} %get-tuple-element.8) | copy-start | bytes 6291460

commit v4 on v3

--- a/solution.py
+++ b/solution.py
@@ -30,7 +30,7 @@
 
 def attention_kernel(
     steps, rows, ctx_size, head_size, ahead, behind, score_scale,
-    bounds_ref, q_ref, do_ref, own_ref, o_ref, dq_ref, dkv_ref,
+    bounds_ref, q_ref, do_ref, own_ref, o_ref, dq_ref, dk_ref, dv_ref,
     window, leaving, landed, own_part, bias, q_s, do_s, o_s, dq_s,
     k_s, v_s, kt_s, vt_s, dk_s, dv_s,
     kv_send, kv_recv, d_send, d_recv, row_here, row_send, row_recv, out_here, out_send, out_recv,
@@ -151,7 +151,8 @@
         each_target(add)
         for side in range(2):
             head = side * local_heads + k
-            dkv_ref[head] = own_part[head].astype(dkv_ref.dtype)
+            dk_ref[head] = own_part[head, 0].astype(dk_ref.dtype)
+            dv_ref[head] = own_part[head, 1].astype(dv_ref.dtype)
 
     @pl.when(g == 0)
     def _():
@@ -291,12 +292,14 @@
     slots = steps + 1 + lax.axis_size("head")
     reach = slots * tokens
     total_rows = tokens * width
-    rows = min(256, total_rows)
+    rows = min(1024, total_rows)
     q4 = queries.reshape(tokens, kv_count, width, size_head)
     do4 = output_gradient.reshape(tokens, kv_count, width, size_head)
     anywhere = pl.BlockSpec(memory_space=pl.ANY)
     row_shape = jax.ShapeDtypeStruct(q4.shape, jnp.bfloat16)
     full = pl.BlockSpec(own.shape, lambda g: (0, 0, 0, 0))
+    half = pl.BlockSpec((kv_count, tokens, size_head), lambda g: (0, 0, 0))
+    half_shape = jax.ShapeDtypeStruct((kv_count, tokens, size_head), jnp.bfloat16)
     row_buffer = pltpu.VMEM((local_heads, 2, tokens, width, size_head), jnp.bfloat16)
     pair = pltpu.SemaphoreType.DMA((local_heads, 2))
     outs = pl.pallas_call(
@@ -306,14 +309,14 @@
             rows,
             lax.axis_size("ctx"),
             lax.axis_size("head"),
-            min(2, local_heads),
+            min(4, local_heads),
             min(2, local_heads - 1),
             score_scale,
         ),
         grid=(local_heads,),
         in_specs=[pl.BlockSpec((4, total_rows), lambda g: (0, 0)), anywhere, anywhere, full],
-        out_specs=[anywhere, anywhere, full],
-        out_shape=[row_shape, row_shape, jax.ShapeDtypeStruct(own.shape, jnp.bfloat16)],
+        out_specs=[anywhere, anywhere, half, half],
+        out_shape=[row_shape, row_shape, half_shape, half_shape],
         scratch_shapes=[
             pltpu.VMEM((local_heads, slots) + own.shape[1:], jnp.bfloat16),
             pltpu.VMEM((local_heads, slots) + own.shape[1:], jnp.bfloat16),
@@ -349,7 +352,7 @@
         ),
         name="attention",
     )(bounds, q4, do4, own)
-    return outs[0].reshape(queries.shape), outs[1].reshape(queries.shape), outs[2]
+    return outs[0].reshape(queries.shape), outs[1].reshape(queries.shape), outs[2], outs[3]
 
 
 def body(queries, key_heads, head_values, output_gradient, doc_lengths):
@@ -367,11 +370,12 @@
         bounds += [document_starts(doc_lengths, query_pos) - window_base, query_pos - window_base]
     bounds = jnp.repeat(jnp.stack(bounds, 0), width, axis=1)
     own = jnp.transpose(jnp.stack([key_heads, head_values], 0), (2, 0, 1, 3))
-    attended, grad_query, total = attention(
+    attended, grad_query, grad_keys, grad_values = attention(
         queries, output_gradient, own, bounds, steps, size_head ** (-0.5)
     )
-    total = jnp.transpose(total, (1, 2, 0, 3))
-    return attended, grad_query, total[0], total[1]
+    grad_keys = jnp.transpose(grad_keys, (1, 0, 2))
+    grad_values = jnp.transpose(grad_values, (1, 0, 2))
+    return attended, grad_query, grad_keys, grad_values
 
 
 def solution(mesh):

time: 106 us -> 90 us (0.85)
  Pallas kernels: 93.6 us -> 76.3 us
  local copies, waits for them, and re-layouts: 8.65 us -> 10.2 us
    pallas_call x1, Pallas kernels: 93.6 us -> 76.3 us  [attention(): pl.pallas_call(functools.partial(attention_kernel, steps, rows, lax.axis_...]
    unnamed x8 -> x6, local copies, waits for them, and re-layouts: 5.42 us -> 8.2 us
    squeeze x1 -> x0, local copies, waits for them, and re-layouts: 1.22 us -> none  [body(): return (attended, grad_query, total[0], total[1])]
where the time goes in v4:
time: 90 us; the launch traced here: 89.6 us
  Pallas kernels  76.3 us (85%)
  local copies, waits for them, and re-layouts  10.2 us (11%)
  other arithmetic  2.44 us (3%)
    pallas_call x1, Pallas kernels, attention(): pl.pallas_call(functools.partial(attention_kernel, steps, rows, lax.axis_...  76.3 us
    unnamed x6, local copies, waits for them, and re-layouts  8.2 us

profile of v4, /device:TPU:23, one launch (start us, length us, event | category | flops | bytes accessed | tf_op | source)
XLA Modules:
  0.0 89.6 jit_solution(9481162600903294275)
XLA Ops:
  0.6 0.8 reduce-window.8
  1.5 0.7 select_reduce_fusion.1
  2.3 0.1 broadcast_in_dim.27
  2.4 0.8 reshape.96.bounds_ref
  3.2 1.1 %copy_bitcast_fusion = (bf16[1,128,8,128]{3,1,0,2:T(8,128)(2,1)S(1)}, bf16[1,128,8,128]{3,1,0,2:T(8,128)(2,1)S(1)}) fusion(bf16[128,8,128]{2,1,0:T(8,128)(2,1)} %param.7, bf16[128,8,128]{2,1,0:T(8,128)(2,1)} %param.6), kind=kLoop, calls=%fused_computation.1 | loop fusion | bytes 1048576 | tf_op jit(solution)/shard_map/stack | solution.py:372
  4.3 0.8 maximum_bitcast_fusion.own_ref
  5.1 76.3 %attention.1 = (bf16[128,8,8,128]{3,2,1,0:T(8,128)(2,1)}, bf16[128,8,8,128]{3,2,1,0:T(8,128)(2,1)}, bf16[8,128,128]{2,1,0:T(8,128)(2,1)}, bf16[8,128,128]{2,1,0:T(8,128)(2,1)}) custom-call(s32[4,1024]{1,0:T(4,128)} %reshape.96.bounds_ref, bf16[128,8,8,128]{3,2,1,0:T(8,128)(2,1)} %bitcast.18, bf16[128,8,8,128]{3,2,1,0:T(8,128)(2,1)} %bitcast.19, ...), custom_call_target="tpu_custom_call" | custom-call | tf_op jit(solution)/shard_map/attention/pallas_call | solution.py:305
  81.4 1.8 %copy.19 = bf16[128,8,128]{2,1,0:T(8,128)(2,1)} copy(bf16[128,8,128]{2,0,1:T(8,128)(2,1)} %bitcast.23) | data formatting | bytes 524288
  83.3 1.8 %copy.20 = bf16[128,8,128]{2,1,0:T(8,128)(2,1)} copy(bf16[128,8,128]{2,0,1:T(8,128)(2,1)} %bitcast.22) | data formatting | bytes 524288
  85.1 0.0 copy-start
  85.1 3.2 %copy.25 = bf16[128,64,128]{2,1,0:T(8,128)(2,1)} copy(bf16[128,64,128]{2,1,0:T(8,128)(2,1)} %bitcast.21) | data formatting | bytes 4194304
  88.3 0.0 copy-done
  88.3 1.3 %copy.26 = bf16[128,64,128]{2,1,0:T(8,128)(2,1)} copy(bf16[128,64,128]{2,1,0:T(8,128)(2,1)S(1)} %bitcast.20) | data formatting | bytes 4194304
  (5 shorter events, 0.0 us)
Async XLA Ops:
  85.1 3.2 %copy-start = (bf16[128,8,8,128]{3,2,1,0:T(8,128)(2,1)S(1)}, bf16[128,8,8,128]{3,2,1,0:T(8,128)(2,1)}, u32[]{:S(2)}) copy-start(bf16[128,8,8,128]{3,2,1,0:T(8,128)(2,1)} %get-tuple-element.9) | copy-start | bytes 6291460
